TPU v7x, 128 devices: a whole 4x4x4 slice. The times are simulated.
128 devices in a mesh: leaf: 128 (over y, z, x, core).
Axes of the slice: x: 4, y: 4, z: 4, core: 2. Of those that a mesh axis runs over, the one named last changes fastest.
Arguments:
- points: float32 [16, 262144], P(None, 'leaf'), may hold values from -6 to 6
- charges: float32 [16, 262144], P(None, 'leaf'), may hold values from -0.6 to 0.6
- near_list: int32 [512, 32], P('leaf'), may hold values from 0 to 511, as said below
- near_count: int32 [512], P('leaf'), may hold values from 1 to 32, as said below
- leaf_basis: float32 [262144, 256], P('leaf'), may hold values from -0.75 to 0.75
- device_basis: float32 [131072, 256], P('leaf'), may hold values from -0.1875 to 0.1875
- device_skeleton: int32 [128, 256], P('leaf'), may hold values from 0 to 2047, as said below
- group_basis: float32 [1024, 8192], P(None, 'leaf'), may hold values from -0.1875 to 0.1875
- group_skeleton: int32 [8192], P('leaf'), may hold values from 0 to 1023, as said below
- cluster_basis: float32 [1024, 2048], P(None, 'leaf'), may hold values from -0.1875 to 0.1875
- cluster_skeleton: int32 [2048], P('leaf'), may hold values from 0 to 1023, as said below
Outputs:
- potentials: float32 [16, 262144], P(None, 'leaf')
Inputs may be any that keep to these rules, and one draw needn't show every extreme that they name: `near_list`: row l names leaves whose devices lie at most 8 devices from leaf l's device; its first entry is l, its first near_count[l] entries are distinct, and the later entries repeat l. Only the first near_count[l] entries of leaf l's list count. `device_skeleton`: each row holds distinct indices into its device's points. `group_skeleton`: entries g * 256 to (g + 1) * 256 - 1 are distinct indices into the 1024 skeleton points of group g's four devices, side by side in device order. `cluster_skeleton`: entries c * 256 to (c + 1) * 256 - 1 are distinct indices into the 1024 skeleton points of cluster c's four groups, side by side in group order.
All inputs are finite; a program needn't handle non-finite values.
Results may differ from a plain program's by a relative error of at most 0.0034.
Values sent between devices are 32-bit elements; how exact they have to be, the bound alone decides.
No kernel may reach another device: no remote copies, remote signals or barrier semaphores. Data moves between devices by JAX's collectives and lax.ppermute only.
A program may use at most 64 MiB of HBM per device.

v0:
```python
import jax
import jax.numpy as jnp
from jax import lax
from jax.experimental import pallas as pl
from jax.experimental.pallas import tpu as pltpu
from jax.sharding import PartitionSpec as P


F = 16
R = 16
LEAF = 512
S = 256
NBR = 32
LEAVES_DEV = 4
PTS = LEAVES_DEV * LEAF
INFO = 128
SKEL_LANE = 68
POINT_SCALE = 0.42466090014400953
UNROLL = 4

f32 = jnp.float32
bf16 = jnp.bfloat16

NN = (((1,), (0,)), ((), ()))
NT = (((1,), (1,)), ((), ()))


def partner(value, mask):
    size = lax.axis_size("leaf")
    return lax.ppermute(value, "leaf", [(source, source ^ mask) for source in range(size)])


def staggered(value, step):
    size = lax.axis_size("leaf")
    pairs = [
        (source, (source + (step if source // step % 2 else -step)) % size)
        for source in range(size)
    ]
    return lax.ppermute(value, "leaf", pairs)


def call(body, outs, args, smem=(), hbm=(), scratch=(), smem_outs=(), aliases=None):
    spaces = [
        pltpu.SMEM if i in smem else pltpu.HBM if i in hbm else pltpu.VMEM
        for i in range(len(args))
    ]
    args = [
        pltpu.with_memory_space_constraint(arg, pltpu.HBM) if i in hbm else arg
        for i, arg in enumerate(args)
    ]
    return pl.pallas_call(
        body,
        out_shape=tuple(outs),
        in_specs=[pl.BlockSpec(memory_space=space) for space in spaces],
        out_specs=tuple(
            pl.BlockSpec(memory_space=pltpu.SMEM if i in smem_outs else pltpu.VMEM)
            for i in range(len(outs))
        ),
        input_output_aliases=aliases or {},
        scratch_shapes=list(scratch),
        compiler_params=pltpu.CompilerParams(vmem_limit_bytes=24 << 20),
    )(*args)


def out(*shape):
    return jax.ShapeDtypeStruct(shape, f32)


def split2(x):
    high = x.astype(bf16)
    return high, (x - high.astype(f32)).astype(bf16)


def split3(x):
    high = x.astype(bf16)
    rest = x - high.astype(f32)
    middle = rest.astype(bf16)
    return high, middle, (rest - middle.astype(f32)).astype(bf16)


def dot(a, b, dims):
    return lax.dot_general(a, b, dims, preferred_element_type=f32)


def product(a, b, dims):
    ah, al = split2(a)
    bh, bl = split2(b)
    rows = a.shape[0]
    both = dot(jnp.concatenate([ah, al], 0), bh, dims)
    return both[:rows] + both[rows:] + dot(ah, bl, dims)


def pick(points, one_hot, dims):
    parts = dot(jnp.concatenate(split3(points), 0), one_hot, dims)
    return parts[:F] + parts[F : 2 * F] + parts[2 * F :]


def one_hot_rows(index_column, first, width):
    lanes = lax.broadcasted_iota(jnp.int32, (index_column.shape[0], width), 1)
    return jnp.where(lanes + first == index_column.astype(jnp.int32), 1.0, 0.0).astype(bf16)


def exponent_rows(points, left):
    scaled = points * POINT_SCALE
    h, m, l = split3(scaled)
    n = points.shape[1]
    nh, nm, nl = split3(-0.5 * jnp.sum(scaled * scaled, axis=0, keepdims=True))
    row = lax.broadcasted_iota(jnp.int32, (16, n), 0)
    first = 0 if left else 3
    block = jnp.where((row >= 3 - first) & (row < 6 - first), 1.0, 0.0)
    for i, part in enumerate((nh, nm, nl)):
        block = jnp.where(row == first + i, part.astype(f32), block)
    block = block.astype(bf16)
    zero = jnp.zeros((16, n), bf16)
    if left:
        return jnp.concatenate([h, h, m, m, h, l, block, zero], 0)
    return jnp.concatenate([h, m, h, m, l, h, block, zero], 0)


SPAN = PTS + INFO
BLOCK = S + INFO


def cluster_block(ref, row, cbt, cskel, gk):
    ref[row : row + 16, :S] = cbt[:, pl.ds(pl.multiple_of(gk * S, S), S)]
    ref[row : row + 16, S:] = cskel


def skeleton_column(row_ref, count, tile):
    tile[...] = jnp.zeros((8, 128), f32)
    tile[0:1, :count] = row_ref[:, :count].astype(f32)
    return jnp.transpose(tile[...])


def pack_first(
    points, charges, near_list, near_count, gskel, cskel, gbt, cbt,
    w, w8, x1, urgent, gkeep, ckeep, csend,
    tile, lists, counts, grow, crow, group, cluster, sems,
):
    d = lax.axis_index("leaf")
    pos = d & 3
    gk = (d >> 2) & 3
    small = [
        pltpu.make_async_copy(source, target, sems.at[i])
        for i, (source, target) in enumerate(
            (
                (near_list, lists),
                (near_count, counts),
                (gskel, grow),
                (cskel, crow),
                (gbt, group),
                (cbt, cluster),
            )
        )
    ]
    cols = pl.ds(0, PTS)
    large = [
        pltpu.make_async_copy(source, target, sems.at[6 + i])
        for i, (source, target) in enumerate(
            (
                (points, w.at[pl.ds(0, F)]),
                (charges, w.at[pl.ds(F, R)]),
                (points, w8.at[pl.ds(0, F), cols]),
                (charges, w8.at[pl.ds(F, R), cols]),
                (points, x1.at[:, cols]),
            )
        )
    ]
    for copy in small + large:
        copy.start()
    x1[:, PTS:SPAN] = jnp.zeros((F, INFO), f32)
    for copy in small:
        copy.wait()
    x1[:4, PTS : PTS + NBR] = lists[...].astype(f32)
    for l in range(LEAVES_DEV):
        x1[l : l + 1, PTS + NBR : PTS + NBR + 1] = jnp.full((1, 1), counts[l], jnp.int32).astype(f32)
    column = skeleton_column(grow, 64, tile)
    for j in range(4):
        lane = PTS + SKEL_LANE + j
        x1[:, lane : lane + 1] = column[16 * j : 16 * j + 16, :1]
    for ref, start, mask in ((x1, SPAN, 1), (x1, SPAN + 4 * S, 3), (gkeep, 0, 0), (urgent, 0, 2)):
        lane = pl.multiple_of((pos ^ mask) * S, S)
        for j in range(4):
            at = start + j * S
            ref[:, at : at + S] = group[16 * j : 16 * j + 16, pl.ds(lane, S)]
    column = jnp.broadcast_to(skeleton_column(crow, 16, tile)[:16, :1], (16, INFO))
    for half, mask in ((0, 2), (16, 3)):
        lane = pl.multiple_of((gk ^ mask) * S, S)
        w8[half : half + 16, PTS : PTS + S] = cluster[:, pl.ds(lane, S)]
        w8[half : half + 16, PTS + S :] = column
    cluster_block(ckeep, 0, cluster, column, gk)
    cluster_block(csend, 0, cluster, column, gk ^ 1)
    for copy in large:
        copy.wait()


def device_up(w, leaf_hbm, device_hbm, skeleton, pay, leaf, device, sems):
    copies = []
    for l in range(LEAVES_DEV):
        rows = pl.ds(l * LEAF, LEAF)
        copies.append(pltpu.make_async_copy(leaf_hbm.at[rows], leaf.at[rows], sems.at[l]))
    last = pltpu.make_async_copy(device_hbm, device, sems.at[LEAVES_DEV])
    for copy in copies:
        copy.start()
    last.start()
    rows = lax.broadcasted_iota(jnp.int32, (PTS, S), 0)
    one_hot = jnp.where(rows == skeleton[...], 1.0, 0.0).astype(bf16)
    pay[:F] = pick(w[:F], one_hot, NN)
    weights = []
    for l in range(LEAVES_DEV):
        copies[l].wait()
        weights.append(
            product(w[F:, l * LEAF : (l + 1) * LEAF], leaf[l * LEAF : (l + 1) * LEAF], NN)
        )
    last.wait()
    pay[F:] = product(jnp.concatenate(weights, 1), device[...], NN)


def group_up(pay, x1, x1r, urgent, gkeep, ckeep, w8r, c2r, e1, rgbt, skel):
    pos = lax.axis_index("leaf") & 3
    sources = (
        (0, gkeep, 0, x1, PTS),
        (1, x1r, SPAN, x1r, PTS),
        (2, urgent, 0, urgent, 8 * S),
        (3, urgent, 4 * S, urgent, 8 * S + INFO),
    )
    for mask, ref, at, info, info_at in sources:
        first = (pos ^ mask) * 64
        for j in range(4):
            row = pl.multiple_of(first + 16 * j, 16)
            rgbt[pl.ds(row, 16), :] = ref[:, at + j * S : at + (j + 1) * S]
            lane = info_at + SKEL_LANE + j
            skel[pl.ds(row, 16), :] = jnp.broadcast_to(info[:, lane : lane + 1], (16, 128))
    e1[:F, :S] = pick(pay[:F], one_hot_rows(skel[:, :1], pos * S, S), NT)
    e1[F:32, :S] = product(pay[F:], rgbt[...], NT)
    e1[:32, S:] = jnp.zeros((32, INFO), f32)
    e1[32:48] = ckeep[...]
    e1[48:64] = w8r[:16, PTS:]
    e1[64:96] = c2r[...]


CLUSTER_MASKS = (0, 8, 6, 14)


def cluster_up(e1, r1, r2, r3, e2, rcbt, skel):
    d = lax.axis_index("leaf")
    gk = (d >> 2) & 3
    for m, ref in enumerate((e1, r1, r2, r3)):
        for b, mask in enumerate(CLUSTER_MASKS):
            row = pl.multiple_of(((d & 15) ^ mask ^ m) * 16, 16)
            rcbt[pl.ds(row, 16), :] = ref[32 + 16 * b : 48 + 16 * b, :S]
            skel[pl.ds(row, 16), :] = ref[32 + 16 * b : 48 + 16 * b, S:]
    group = e1[:32, :S] + r1[:32, :S] + (r2[:32, :S] + r3[:32, :S])
    e2[:, :S] = group
    e2[:F, S:] = pick(group[:F], one_hot_rows(skel[:, :1], gk * S, S), NT)
    e2[F:, S:] = product(group[F:], rcbt[...], NT)


def cluster_sum(e2, r1, r2, r3, cpay):
    cpay[...] = e2[:, S:] + r1[:, S:] + (r2[:, S:] + r3[:, S:])


def interact(left, other_points, other_weights):
    values = jnp.exp2(dot(left, exponent_rows(other_points, False), NN))
    return product(other_weights, values, NT)


def early_field(e2, g1, g2, g3, cpay, c1, c2, side, top):
    left = jnp.transpose(exponent_rows(e2[:F, :S], True))
    side[...] = interact(
        left,
        jnp.concatenate([g1[:F, :S], g2[:F, :S], g3[:F, :S]], 1),
        jnp.concatenate([g1[F:, :S], g2[F:, :S], g3[F:, :S]], 1),
    )
    left = jnp.transpose(exponent_rows(cpay[:F], True))
    top[...] = interact(
        left, jnp.concatenate([c1[:F], c2[:F]], 1), jnp.concatenate([c1[F:], c2[F:]], 1)
    )


def downward(cpay, c3, side, top, rcbt, rgbt, device, leaf, far):
    left = jnp.transpose(exponent_rows(cpay[:F], True))
    total = top[...] + interact(left, c3[:F], c3[F:])
    down_group = side[...] + product(total, rcbt[...], NN)
    down_device = product(down_group, rgbt[...], NN)
    down_leaves = product(down_device, device[...], NT)
    for l in range(LEAVES_DEV):
        far[:, l * LEAF : (l + 1) * LEAF] = product(
            down_leaves[:, l * S : (l + 1) * S], leaf[l * LEAF : (l + 1) * LEAF], NT
        )


def make_work(info, work, place):
    d = lax.axis_index("leaf")
    pos = d & 3
    even8 = 1 - ((d >> 3) & 1)
    even4 = 1 - ((d >> 2) & 1)
    place[0] = 1 + even8
    place[1] = 3 + even4
    place[2] = 0
    place[3] = 4 - even4
    place[4] = 2 - even8

    def list_leaf(leaf, filled):
        def list_slot(slot, filled):
            source = info[leaf, slot]
            owner = source >> 2
            mine = (owner & 3) == pos
            shard = place[jnp.where(mine, (owner - d + 8) >> 2, 0)]
            work[filled] = ((shard * 4 + (source & 3)) << 4) | leaf
            return filled + jnp.where(mine, 1, 0)

        return lax.fori_loop(0, info[leaf, NBR], list_slot, filled)

    return lax.fori_loop(0, 16, list_leaf, 0)


def run_tiles(first, last, work, left, right, charge, acc):
    def tile(n):
        item = work[n]
        source = item >> 4
        target = item & 15
        values = jnp.exp2(dot(left[source], right[target], NN)).astype(bf16)
        acc[target] += dot(charge[source], values, NN)

    def several(step, _):
        for u in range(UNROLL):
            tile(first + step * UNROLL + u)
        return 0

    whole = (last - first) // UNROLL
    lax.fori_loop(0, whole, several, 0)

    def single(n, _):
        tile(n)
        return 0

    lax.fori_loop(first + whole * UNROLL, last, single, 0)


PARTS = (0, 6, 11, 16)


def bounds(count, part):
    first = ((count * PARTS[part]) >> 4) & -UNROLL
    last = (count * PARTS[part + 1]) >> 4
    return first, last if part == len(PARTS) - 2 else last & -UNROLL


def near_start(info, w, w8, i8, w4, i4, x1r, targets, acc, left, right, charge, work, place):
    count = make_work(info, work, place)
    work[WORK - 1] = count
    for i, ref in enumerate((w, w8, i8, w4, i4)):
        for l in range(LEAVES_DEV):
            cols = slice(l * LEAF, (l + 1) * LEAF)
            left[4 * i + l] = jnp.transpose(exponent_rows(ref[:F, cols], True))
            charge[4 * i + l] = ref[F:, cols].astype(bf16)
    for q, (ref, at) in enumerate(((w, 0), (x1r, 0), (targets, 0), (targets, SPAN))):
        for l in range(LEAVES_DEV):
            right[4 * q + l] = exponent_rows(ref[:F, at + l * LEAF : at + (l + 1) * LEAF], False)
    acc[...] = jnp.zeros_like(acc)
    run_tiles(*bounds(count, 0), work, left, right, charge, acc)


def near_more(part):
    def body(work, left, right, charge, before, acc):
        del before
        run_tiles(*bounds(work[WORK - 1], part), work, left, right, charge, acc)

    return body


def near_last(work, left, right, charge, before, *parts_acc):
    *parts, acc = parts_acc
    acc[...] = before[...]
    run_tiles(*bounds(work[WORK - 1], len(PARTS) - 2), work, left, right, charge, acc)
    for q, part in enumerate(parts):
        for l in range(LEAVES_DEV):
            part[:, l * LEAF : (l + 1) * LEAF] = acc[4 * q + l]


WORK = 16 * NBR + 16


def program(
    points,
    charges,
    near_list,
    near_count,
    leaf_basis,
    device_basis,
    device_skeleton,
    group_basis,
    group_skeleton,
    cluster_basis,
    cluster_skeleton,
):
    w, w8, x1, urgent, gkeep, ckeep, csend = call(
        pack_first,
        (
            out(32, PTS),
            out(32, PTS + BLOCK),
            out(16, SPAN + 8 * S),
            out(16, 4 * S),
            out(16, 4 * S),
            out(16, BLOCK),
            out(16, BLOCK),
        ),
        (
            points,
            charges,
            near_list,
            near_count,
            group_skeleton.reshape(1, 64),
            cluster_skeleton.reshape(1, 16),
            group_basis.T,
            cluster_basis.T,
        ),
        hbm=range(8),
        scratch=(
            pltpu.VMEM((8, 128), f32),
            pltpu.VMEM((LEAVES_DEV, NBR), jnp.int32),
            pltpu.SMEM((LEAVES_DEV,), jnp.int32),
            pltpu.VMEM((1, 64), jnp.int32),
            pltpu.VMEM((1, 16), jnp.int32),
            pltpu.VMEM((64, 4 * S), f32),
            pltpu.VMEM((16, 4 * S), f32),
            pltpu.SemaphoreType.DMA((11,)),
        ),
    )
    x1r = partner(x1, 1)
    w4r = partner(w, 4)
    w8r = partner(w8, 8)
    i8r = staggered(w, 8)
    i4r = staggered(w, 4)
    urgent = jnp.concatenate([urgent, x1r[:, SPAN + 4 * S :], x1[:, PTS:SPAN], x1r[:, PTS:SPAN]], 1)
    targets = jnp.concatenate([x1[:, :SPAN], x1r[:, :SPAN]], 1)
    urgent = partner(urgent, 2)
    targets = partner(targets, 2)
    (pay,) = call(
        device_up,
        (out(32, S),),
        (w, leaf_basis, device_basis, device_skeleton),
        hbm=(1, 2),
        scratch=(
            pltpu.VMEM((PTS, S), f32),
            pltpu.VMEM((LEAVES_DEV * S, S), f32),
            pltpu.SemaphoreType.DMA((LEAVES_DEV + 1,)),
        ),
    )
    c2r = partner(jnp.concatenate([csend, w8r[16:, PTS:]], 0), 6)
    e1, rgbt, _ = call(
        group_up,
        (out(96, BLOCK), out(S, S), out(S, 128)),
        (pay, x1, x1r, urgent, gkeep, ckeep, w8r, c2r),
    )
    g1, g2, g3 = (partner(e1, m) for m in (1, 2, 3))
    e2, rcbt, _ = call(cluster_up, (out(32, 2 * S), out(S, S), out(S, 128)), (e1, g1, g2, g3))
    h1, h2, h3 = (partner(e2, m) for m in (8, 6, 14))
    (cpay,) = call(cluster_sum, (out(32, S),), (e2, h1, h2, h3))
    c1 = partner(cpay, 24)
    pair = jnp.concatenate([cpay, c1], 1)
    c2 = partner(pair, 32)
    c3 = partner(jnp.concatenate([pair, c2], 1), 96)
    side, top = call(early_field, (out(16, S), out(16, S)), (e2, h1, h2, h3, cpay, c1, c2))

    info = jnp.concatenate(
        [
            x1[:4, PTS:SPAN],
            x1r[:4, PTS:SPAN],
            targets[:4, PTS:SPAN],
            targets[:4, SPAN + PTS :],
        ],
        0,
    ).astype(jnp.int32)
    acc, left, right, charge, work = call(
        near_start,
        (
            out(16, R, LEAF),
            jax.ShapeDtypeStruct((20, LEAF, 128), bf16),
            jax.ShapeDtypeStruct((16, 128, LEAF), bf16),
            jax.ShapeDtypeStruct((20, R, LEAF), bf16),
            jax.ShapeDtypeStruct((WORK,), jnp.int32),
        ),
        (info, w, w8r, i8r, w4r, i4r, x1r, targets),
        smem=(0,),
        smem_outs=(4,),
        scratch=(pltpu.SMEM((8,), jnp.int32),),
    )
    for part in range(1, len(PARTS) - 2):
        (acc,) = call(
            near_more(part),
            (out(16, R, LEAF),),
            (work, left, right, charge, acc),
            smem=(0,),
            aliases={4: 0},
        )
    n0, n1, n2, n3 = call(
        near_last,
        (out(R, PTS),) * 4,
        (work, left, right, charge, acc),
        smem=(0,),
        scratch=(pltpu.VMEM((16, R, LEAF), f32),),
    )
    n3 = partner(n3, 3)
    n2 = partner(n2, 2)
    n1 = partner(n1, 1)
    (far,) = call(
        downward, (out(16, PTS),), (cpay, c3, side, top, rcbt, rgbt, device_basis, leaf_basis)
    )
    return n0 + n1 + (n2 + n3) + far


def solution(mesh):
    return jax.shard_map(
        program,
        mesh=mesh,
        in_specs=(
            P(None, "leaf"),
            P(None, "leaf"),
            P("leaf", None),
            P("leaf"),
            P("leaf", None),
            P("leaf", None),
            P("leaf", None),
            P(None, "leaf"),
            P("leaf"),
            P(None, "leaf"),
            P("leaf"),
        ),
        out_specs=P(None, "leaf"),
        check_vma=False,
    )
```

profile of v0, /device:TPU:9, one launch (start us, length us, event | category | flops | bytes accessed | tf_op | source)
XLA Modules:
  0.0 100.7 jit_solution(18161835249212516074)
XLA Ops:
  0.0 1.4 %shard_map.109 = (f32[32,2048]{1,0:T(8,128)S(1)}, f32[32,2432]{1,0:T(8,128)S(1)}, f32[16,4224]{1,0:T(8,128)S(1)}, f32[16,1024]{1,0:T(8,128)S(1)}, f32[16,1024]{1...) custom-call(f32[16,2048]{1,0:T(8,128)} %points.1, f32[16,2048]{1,0:T(8,128)} %charges.1, ...), custom_call_target="tpu_custom_call" | custom-call | tf_op jit(solution)/shard_map/pallas_call | solution.py:51
  2.1 1.6 %collective-permute-start.2 = (f32[32,2432]{1,0:T(8,128)S(1)}, f32[32,2432]{1,0:T(8,128)S(1)}, u32[]{:S(2)}, u32[]{:S(2)}) collective-permute-start(f32[32,2432]{1,0:T(8,128)S(1)} %get-tuple-element.29), channel_id=1, source_target_pairs={{0,8},{1,9},{2,10},{3,11},{4,12},{5,13},{6,14},{7,15},{8,0},{9,1},... | collective-permute-start | bytes 933896 | tf_op jit(solution)/shard_map/ppermute | solution.py:30
  3.9 1.3 %collective-permute-start.9 = (f32[16,2304]{1,0:T(8,128)S(1)}, f32[16,2304]{1,0:T(8,128)S(1)}, u32[]{:S(2)}, u32[]{:S(2)}) collective-permute-start(f32[16,2304]{1,0:T(8,128)S(1)} %pad_maximum_fusion.1), channel_id=1, source_target_pairs={{0,2},{1,3},{2,0},{3,1},{4,6},{5,7},{6,4},{7,5},{8,10},{9,11},{10,... | collective-permute-start | bytes 442376 | tf_op jit(solution)/shard_map/ppermute | solution.py:30
  5.5 5.8 %collective-permute-done.2.w8.w8r = f32[32,2432]{1,0:T(8,128)S(1)} collective-permute-done((f32[32,2432]{1,0:T(8,128)S(1)}, f32[32,2432]{1,0:T(8,128)S(1)}, u32[]{:S(2)}, u32[]{:S(2)}) %collective-permute-start.2) | collective-permute-done | bytes 311328 | tf_op jit(solution)/shard_map/ppermute | solution.py:30
  11.3 2.6 %collective-permute-start.10 = (f32[32,384]{1,0:T(8,128)S(1)}, f32[32,384]{1,0:T(8,128)S(1)}, u32[]{:S(2)}, u32[]{:S(2)}) collective-permute-start(f32[32,384]{1,0:T(8,128)S(1)} %pad_maximum_fusion.4), channel_id=1, source_target_pairs={{0,6},{1,7},{2,4},{3,5},{4,2},{5,3},{6,0},{7,1},{8,14},{9,15},{10,... | collective-permute-start | bytes 147464 | tf_op jit(solution)/shard_map/ppermute | solution.py:30
  13.9 2.5 %shard_map.113.pay = f32[32,256]{1,0:T(8,128)S(1)} custom-call(f32[32,2048]{1,0:T(8,128)S(1)} %get-tuple-element.28.w, f32[2048,256]{1,0:T(8,128)} %leaf.1, f32[1024,256]{1,0:T(8,128)} %device.1, s32[1,256]{1,0:T(1,128)S(1)} %copy-done.2), custom_call_target="tpu_custom_call" | custom-call | tf_op jit(solution)/shard_map/pallas_call | solution.py:51
  16.4 0.8 shard_map.114
  17.2 1.0 collective-permute-start.13
  18.1 1.5 %collective-permute-start.12 = (f32[96,384]{1,0:T(8,128)S(1)}, f32[96,384]{1,0:T(8,128)S(1)}, u32[]{:S(2)}, u32[]{:S(2)}) collective-permute-start(f32[96,384]{1,0:T(8,128)S(1)} %get-tuple-element.43.e1), channel_id=1, source_target_pairs={{0,2},{1,3},{2,0},{3,1},{4,6},{5,7},{6,4},{7,5},{8,10},{9,11},{10,... | collective-permute-start | bytes 442376 | tf_op jit(solution)/shard_map/ppermute | solution.py:30
  19.6 3.6 %collective-permute-done.13.r3 = f32[96,384]{1,0:T(8,128)S(1)} collective-permute-done((f32[96,384]{1,0:T(8,128)S(1)}, f32[96,384]{1,0:T(8,128)S(1)}, u32[]{:S(2)}, u32[]{:S(2)}) %collective-permute-start.13) | collective-permute-done | bytes 147488 | tf_op jit(solution)/shard_map/ppermute | solution.py:30
  23.2 3.3 %collective-permute-done.12.r2 = f32[96,384]{1,0:T(8,128)S(1)} collective-permute-done((f32[96,384]{1,0:T(8,128)S(1)}, f32[96,384]{1,0:T(8,128)S(1)}, u32[]{:S(2)}, u32[]{:S(2)}) %collective-permute-start.12) | collective-permute-done | bytes 147488 | tf_op jit(solution)/shard_map/ppermute | solution.py:30
  27.2 2.6 %collective-permute-start.16 = (f32[32,512]{1,0:T(8,128)S(1)}, f32[32,512]{1,0:T(8,128)S(1)}, u32[]{:S(2)}, u32[]{:S(2)}) collective-permute-start(f32[32,512]{1,0:T(8,128)S(1)} %get-tuple-element.44.e2), channel_id=1, source_target_pairs={{0,14},{1,15},{2,12},{3,13},{4,10},{5,11},{6,8},{7,9},{8,6},{9,7},... | collective-permute-start | bytes 196616 | tf_op jit(solution)/shard_map/ppermute | solution.py:30
  29.8 1.0 %collective-permute-start.15 = (f32[32,512]{1,0:T(8,128)S(1)}, f32[32,512]{1,0:T(8,128)S(1)}, u32[]{:S(2)}, u32[]{:S(2)}) collective-permute-start(f32[32,512]{1,0:T(8,128)S(1)} %get-tuple-element.44.e2), channel_id=1, source_target_pairs={{0,6},{1,7},{2,4},{3,5},{4,2},{5,3},{6,0},{7,1},{8,14},{9,15},{10,... | collective-permute-start | bytes 196616 | tf_op jit(solution)/shard_map/ppermute | solution.py:30
  31.0 3.2 %collective-permute-start.5 = (f32[32,2048]{1,0:T(8,128)S(1)}, f32[32,2048]{1,0:T(8,128)S(1)}, u32[]{:S(2)}, u32[]{:S(2)}) collective-permute-start(f32[32,2048]{1,0:T(8,128)S(1)} %get-tuple-element.28.w), channel_id=1, source_target_pairs={{0,124},{1,125},{2,126},{3,127},{4,8},{5,9},{6,10},{7,11},{8,4},{9... | collective-permute-start | bytes 786440 | tf_op jit(solution)/shard_map/ppermute | solution.py:39
  35.0 2.3 %collective-permute-start.3 = (f32[32,2048]{1,0:T(8,128)S(1)}, f32[32,2048]{1,0:T(8,128)S(1)}, u32[]{:S(2)}, u32[]{:S(2)}) collective-permute-start(f32[32,2048]{1,0:T(8,128)S(1)} %get-tuple-element.28.w), channel_id=1, source_target_pairs={{0,120},{1,121},{2,122},{3,123},{4,124},{5,125},{6,126},{7,127},{8... | collective-permute-start | bytes 786440 | tf_op jit(solution)/shard_map/ppermute | solution.py:39
  37.3 1.5 %collective-permute-start.17 = (f32[32,256]{1,0:T(8,128)S(1)}, f32[32,256]{1,0:T(8,128)S(1)}, u32[]{:S(2)}, u32[]{:S(2)}) collective-permute-start(f32[32,256]{1,0:T(8,128)S(1)} %shard_map.116.cpay), channel_id=1, source_target_pairs={{0,24},{1,25},{2,26},{3,27},{4,28},{5,29},{6,30},{7,31},{8,16},{9,... | collective-permute-start | bytes 98312 | tf_op jit(solution)/shard_map/ppermute | solution.py:30
  38.8 11.3 %collective-permute-done.17.c1 = f32[32,256]{1,0:T(8,128)S(1)} collective-permute-done((f32[32,256]{1,0:T(8,128)S(1)}, f32[32,256]{1,0:T(8,128)S(1)}, u32[]{:S(2)}, u32[]{:S(2)}) %collective-permute-start.17) | collective-permute-done | bytes 32800 | tf_op jit(solution)/shard_map/ppermute | solution.py:30
  50.1 1.5 %collective-permute-start.18 = (f32[32,512]{1,0:T(8,128)S(1)}, f32[32,512]{1,0:T(8,128)S(1)}, u32[]{:S(2)}, u32[]{:S(2)}) collective-permute-start(f32[32,512]{1,0:T(8,128)S(1)} %pad_maximum_fusion.3), channel_id=1, source_target_pairs={{0,32},{1,33},{2,34},{3,35},{4,36},{5,37},{6,38},{7,39},{8,40},{9,... | collective-permute-start | bytes 196616 | tf_op jit(solution)/shard_map/ppermute | solution.py:30
  51.6 18.6 %shard_map.110 = (f32[16,16,512]{2,1,0:T(8,128)S(1)}, bf16[20,512,128]{2,1,0:T(8,128)(2,1)S(1)}, bf16[16,128,512]{2,1,0:T(8,128)(2,1)S(1)}, bf16[20,16,512]{2,1,0:T(8,128)(2,1)S(1)}, s32[528]{0:T(1024)S(1)}) custom-call(s32[16,128]{1,0:T(8,128)S(1)} %maximum_convert_fusion.info, f32[32,2048]{1,0:T(8,128)S(1)} %get-tuple-element.28.w, ...), custom_call_target="tpu_custom_call" | custom-call | tf_op jit(solution)/shard_map/pallas_call | solution.py:51
  70.3 10.7 %shard_map.111.before = f32[16,16,512]{2,1,0:T(8,128)S(1)} custom-call(s32[528]{0:T(1024)S(1)} %get-tuple-element.30.work, bf16[20,512,128]{2,1,0:T(8,128)(2,1)S(1)} %get-tuple-element.31.left, bf16[16,128,512]{2,1,0:T(8,128)(2,1)S(1)} %get-tuple-element.32.right, bf16[20,16,512]{2,1,0:T(8,128)(2,1)S(1)} %get-tuple-element.33.charge, ...), custom_call_target="tpu_custom_call", output_to_operand_aliasing={{}: (4, {})} | custom-call | tf_op jit(solution)/shard_map/pallas_call | solution.py:51
  81.0 10.8 %shard_map.112 = (f32[16,2048]{1,0:T(8,128)S(1)}, f32[16,2048]{1,0:T(8,128)S(1)}, f32[16,2048]{1,0:T(8,128)S(1)}, f32[16,2048]{1,0:T(8,128)S(1)}) custom-call(s32[528]{0:T(1024)S(1)} %get-tuple-element.30.work, bf16[20,512,128]{2,1,0:T(8,128)(2,1)S(1)} %get-tuple-element.31.left, bf16[16,128,512]{2,1,0:T(8,128)(2,1)S(1)} %get-tuple-element.32.right, ...), custom_call_target="tpu_custom_call" | custom-call | tf_op jit(solution)/shard_map/pallas_call | solution.py:51
  92.0 2.0 %collective-permute-start.8 = (f32[16,2048]{1,0:T(8,128)S(1)}, f32[16,2048]{1,0:T(8,128)S(1)}, u32[]{:S(2)}, u32[]{:S(2)}) collective-permute-start(f32[16,2048]{1,0:T(8,128)S(1)} %get-tuple-element.38), channel_id=1, source_target_pairs={{0,3},{1,2},{2,1},{3,0},{4,7},{5,6},{6,5},{7,4},{8,11},{9,10},{10,... | collective-permute-start | bytes 393224 | tf_op jit(solution)/shard_map/ppermute | solution.py:30
  94.8 2.3 %shard_map.118 = f32[16,2048]{1,0:T(8,128)S(1)} custom-call(f32[32,256]{1,0:T(8,128)S(1)} %shard_map.116.cpay, f32[32,1024]{1,0:T(8,128)S(1)} %collective-permute-done.19.c3, f32[16,256]{1,0:T(8,128)S(1)} %get-tuple-element.45.side, f32[16,256]{1,0:T(8,128)S(1)} %get-tuple-element.46.top, f32[256,256]{1,0:T(8,128)S(1)} %get-tuple-element.47.rcbt, ...), custom_call_target="tpu_custom_call" | custom-call | tf_op jit(solution)/shard_map/pallas_call | solution.py:51
  97.1 2.9 %collective-permute-done.8 = f32[16,2048]{1,0:T(8,128)S(1)} collective-permute-done((f32[16,2048]{1,0:T(8,128)S(1)}, f32[16,2048]{1,0:T(8,128)S(1)}, u32[]{:S(2)}, u32[]{:S(2)}) %collective-permute-start.8) | collective-permute-done | bytes 131104 | tf_op jit(solution)/shard_map/ppermute | solution.py:30
  (48 shorter events, 4.6 us)
Async XLA Ops:
  0.0 13.9 %copy-start.2 = (s32[1,256]{1,0:T(1,128)S(1)}, s32[1,256]{1,0:T(1,128)}, u32[]{:S(2)}) copy-start(s32[1,256]{1,0:T(1,128)} %skeleton.1) | copy-start | bytes 3076
  1.4 2.4 %collective-permute-start = (f32[16,4224]{1,0:T(8,128)S(1)}, f32[16,4224]{1,0:T(8,128)S(1)}, u32[]{:S(2)}, u32[]{:S(2)}) collective-permute-start(f32[16,4224]{1,0:T(8,128)S(1)} %get-tuple-element.27.x1), channel_id=1, source_target_pairs={{0,1},{1,0},{2,3},{3,2},{4,5},{5,4},{6,7},{7,6},{8,9},{9,8},{10,11... | collective-permute-start | bytes 811016 | tf_op jit(solution)/shard_map/ppermute | solution.py:30
  2.1 9.2 %collective-permute-start.2 = (f32[32,2432]{1,0:T(8,128)S(1)}, f32[32,2432]{1,0:T(8,128)S(1)}, u32[]{:S(2)}, u32[]{:S(2)}) collective-permute-start(f32[32,2432]{1,0:T(8,128)S(1)} %get-tuple-element.29), channel_id=1, source_target_pairs={{0,8},{1,9},{2,10},{3,11},{4,12},{5,13},{6,14},{7,15},{8,0},{9,1},... | collective-permute-start | bytes 933896 | tf_op jit(solution)/shard_map/ppermute | solution.py:30
  3.9 12.5 %collective-permute-start.9 = (f32[16,2304]{1,0:T(8,128)S(1)}, f32[16,2304]{1,0:T(8,128)S(1)}, u32[]{:S(2)}, u32[]{:S(2)}) collective-permute-start(f32[16,2304]{1,0:T(8,128)S(1)} %pad_maximum_fusion.1), channel_id=1, source_target_pairs={{0,2},{1,3},{2,0},{3,1},{4,6},{5,7},{6,4},{7,5},{8,10},{9,11},{10,... | collective-permute-start | bytes 442376 | tf_op jit(solution)/shard_map/ppermute | solution.py:30
  5.2 33.6 %collective-permute-start.1 = (f32[16,4352]{1,0:T(8,128)S(1)}, f32[16,4352]{1,0:T(8,128)S(1)}, u32[]{:S(2)}, u32[]{:S(2)}) collective-permute-start(f32[16,4352]{1,0:T(8,128)S(1)} %pad_maximum_fusion), channel_id=1, source_target_pairs={{0,2},{1,3},{2,0},{3,1},{4,6},{5,7},{6,4},{7,5},{8,10},{9,11},{10,... | collective-permute-start | bytes 835592 | tf_op jit(solution)/shard_map/ppermute | solution.py:30
  11.3 5.1 %collective-permute-start.10 = (f32[32,384]{1,0:T(8,128)S(1)}, f32[32,384]{1,0:T(8,128)S(1)}, u32[]{:S(2)}, u32[]{:S(2)}) collective-permute-start(f32[32,384]{1,0:T(8,128)S(1)} %pad_maximum_fusion.4), channel_id=1, source_target_pairs={{0,6},{1,7},{2,4},{3,5},{4,2},{5,3},{6,0},{7,1},{8,14},{9,15},{10,... | collective-permute-start | bytes 147464 | tf_op jit(solution)/shard_map/ppermute | solution.py:30
  17.2 6.0 %collective-permute-start.13 = (f32[96,384]{1,0:T(8,128)S(1)}, f32[96,384]{1,0:T(8,128)S(1)}, u32[]{:S(2)}, u32[]{:S(2)}) collective-permute-start(f32[96,384]{1,0:T(8,128)S(1)} %get-tuple-element.43.e1), channel_id=1, source_target_pairs={{0,3},{1,2},{2,1},{3,0},{4,7},{5,6},{6,5},{7,4},{8,11},{9,10},{10,... | collective-permute-start | bytes 442376 | tf_op jit(solution)/shard_map/ppermute | solution.py:30
  18.1 8.3 %collective-permute-start.12 = (f32[96,384]{1,0:T(8,128)S(1)}, f32[96,384]{1,0:T(8,128)S(1)}, u32[]{:S(2)}, u32[]{:S(2)}) collective-permute-start(f32[96,384]{1,0:T(8,128)S(1)} %get-tuple-element.43.e1), channel_id=1, source_target_pairs={{0,2},{1,3},{2,0},{3,1},{4,6},{5,7},{6,4},{7,5},{8,10},{9,11},{10,... | collective-permute-start | bytes 442376 | tf_op jit(solution)/shard_map/ppermute | solution.py:30
  19.6 6.9 %collective-permute-start.11 = (f32[96,384]{1,0:T(8,128)S(1)}, f32[96,384]{1,0:T(8,128)S(1)}, u32[]{:S(2)}, u32[]{:S(2)}) collective-permute-start(f32[96,384]{1,0:T(8,128)S(1)} %get-tuple-element.43.e1), channel_id=1, source_target_pairs={{0,1},{1,0},{2,3},{3,2},{4,5},{5,4},{6,7},{7,6},{8,9},{9,8},{10,11... | collective-permute-start | bytes 442376 | tf_op jit(solution)/shard_map/ppermute | solution.py:30
  27.2 7.1 %collective-permute-start.16 = (f32[32,512]{1,0:T(8,128)S(1)}, f32[32,512]{1,0:T(8,128)S(1)}, u32[]{:S(2)}, u32[]{:S(2)}) collective-permute-start(f32[32,512]{1,0:T(8,128)S(1)} %get-tuple-element.44.e2), channel_id=1, source_target_pairs={{0,14},{1,15},{2,12},{3,13},{4,10},{5,11},{6,8},{7,9},{8,6},{9,7},... | collective-permute-start | bytes 196616 | tf_op jit(solution)/shard_map/ppermute | solution.py:30
  29.8 5.2 %collective-permute-start.15 = (f32[32,512]{1,0:T(8,128)S(1)}, f32[32,512]{1,0:T(8,128)S(1)}, u32[]{:S(2)}, u32[]{:S(2)}) collective-permute-start(f32[32,512]{1,0:T(8,128)S(1)} %get-tuple-element.44.e2), channel_id=1, source_target_pairs={{0,6},{1,7},{2,4},{3,5},{4,2},{5,3},{6,0},{7,1},{8,14},{9,15},{10,... | collective-permute-start | bytes 196616 | tf_op jit(solution)/shard_map/ppermute | solution.py:30
  30.9 6.5 %collective-permute-start.14 = (f32[32,512]{1,0:T(8,128)S(1)}, f32[32,512]{1,0:T(8,128)S(1)}, u32[]{:S(2)}, u32[]{:S(2)}) collective-permute-start(f32[32,512]{1,0:T(8,128)S(1)} %get-tuple-element.44.e2), channel_id=1, source_target_pairs={{0,8},{1,9},{2,10},{3,11},{4,12},{5,13},{6,14},{7,15},{8,0},{9,1},... | collective-permute-start | bytes 196616 | tf_op jit(solution)/shard_map/ppermute | solution.py:30
  31.0 20.5 %collective-permute-start.5 = (f32[32,2048]{1,0:T(8,128)S(1)}, f32[32,2048]{1,0:T(8,128)S(1)}, u32[]{:S(2)}, u32[]{:S(2)}) collective-permute-start(f32[32,2048]{1,0:T(8,128)S(1)} %get-tuple-element.28.w), channel_id=1, source_target_pairs={{0,124},{1,125},{2,126},{3,127},{4,8},{5,9},{6,10},{7,11},{8,4},{9... | collective-permute-start | bytes 786440 | tf_op jit(solution)/shard_map/ppermute | solution.py:39
  34.3 17.3 %collective-permute-start.4 = (f32[32,2048]{1,0:T(8,128)S(1)}, f32[32,2048]{1,0:T(8,128)S(1)}, u32[]{:S(2)}, u32[]{:S(2)}) collective-permute-start(f32[32,2048]{1,0:T(8,128)S(1)} %get-tuple-element.28.w), channel_id=1, source_target_pairs={{0,4},{1,5},{2,6},{3,7},{4,0},{5,1},{6,2},{7,3},{8,12},{9,13},{10,... | collective-permute-start | bytes 786440 | tf_op jit(solution)/shard_map/ppermute | solution.py:30
  35.0 16.6 %collective-permute-start.3 = (f32[32,2048]{1,0:T(8,128)S(1)}, f32[32,2048]{1,0:T(8,128)S(1)}, u32[]{:S(2)}, u32[]{:S(2)}) collective-permute-start(f32[32,2048]{1,0:T(8,128)S(1)} %get-tuple-element.28.w), channel_id=1, source_target_pairs={{0,120},{1,121},{2,122},{3,123},{4,124},{5,125},{6,126},{7,127},{8... | collective-permute-start | bytes 786440 | tf_op jit(solution)/shard_map/ppermute | solution.py:39
  37.3 12.8 %collective-permute-start.17 = (f32[32,256]{1,0:T(8,128)S(1)}, f32[32,256]{1,0:T(8,128)S(1)}, u32[]{:S(2)}, u32[]{:S(2)}) collective-permute-start(f32[32,256]{1,0:T(8,128)S(1)} %shard_map.116.cpay), channel_id=1, source_target_pairs={{0,24},{1,25},{2,26},{3,27},{4,28},{5,29},{6,30},{7,31},{8,16},{9,... | collective-permute-start | bytes 98312 | tf_op jit(solution)/shard_map/ppermute | solution.py:30
  50.1 20.1 %collective-permute-start.18 = (f32[32,512]{1,0:T(8,128)S(1)}, f32[32,512]{1,0:T(8,128)S(1)}, u32[]{:S(2)}, u32[]{:S(2)}) collective-permute-start(f32[32,512]{1,0:T(8,128)S(1)} %pad_maximum_fusion.3), channel_id=1, source_target_pairs={{0,32},{1,33},{2,34},{3,35},{4,36},{5,37},{6,38},{7,39},{8,40},{9,... | collective-permute-start | bytes 196616 | tf_op jit(solution)/shard_map/ppermute | solution.py:30
  70.2 24.5 %collective-permute-start.19 = (f32[32,1024]{1,0:T(8,128)S(1)}, f32[32,1024]{1,0:T(8,128)S(1)}, u32[]{:S(2)}, u32[]{:S(2)}) collective-permute-start(f32[32,1024]{1,0:T(8,128)S(1)} %pad_maximum_fusion.2), channel_id=1, source_target_pairs={{0,96},{1,97},{2,98},{3,99},{4,100},{5,101},{6,102},{7,103},{8,104... | collective-permute-start | bytes 393224 | tf_op jit(solution)/shard_map/ppermute | solution.py:30
  81.0 13.7 %copy-start = (f32[2048,256]{1,0:T(8,128)S(1)}, f32[2048,256]{1,0:T(8,128)}, u32[]{:S(2)}) copy-start(f32[2048,256]{1,0:T(8,128)} %leaf.1) | copy-start | bytes 6291460
  81.0 13.8 %copy-start.1 = (f32[1024,256]{1,0:T(8,128)S(1)}, f32[1024,256]{1,0:T(8,128)}, u32[]{:S(2)}) copy-start(f32[1024,256]{1,0:T(8,128)} %device.1) | copy-start | bytes 3145732
  91.8 5.3 %collective-permute-start.6 = (f32[16,2048]{1,0:T(8,128)S(1)}, f32[16,2048]{1,0:T(8,128)S(1)}, u32[]{:S(2)}, u32[]{:S(2)}) collective-permute-start(f32[16,2048]{1,0:T(8,128)S(1)} %get-tuple-element.36), channel_id=1, source_target_pairs={{0,1},{1,0},{2,3},{3,2},{4,5},{5,4},{6,7},{7,6},{8,9},{9,8},{10,11... | collective-permute-start | bytes 393224 | tf_op jit(solution)/shard_map/ppermute | solution.py:30
  91.9 5.2 %collective-permute-start.7 = (f32[16,2048]{1,0:T(8,128)S(1)}, f32[16,2048]{1,0:T(8,128)S(1)}, u32[]{:S(2)}, u32[]{:S(2)}) collective-permute-start(f32[16,2048]{1,0:T(8,128)S(1)} %get-tuple-element.37), channel_id=1, source_target_pairs={{0,2},{1,3},{2,0},{3,1},{4,6},{5,7},{6,4},{7,5},{8,10},{9,11},{10,... | collective-permute-start | bytes 393224 | tf_op jit(solution)/shard_map/ppermute | solution.py:30
  92.0 8.0 %collective-permute-start.8 = (f32[16,2048]{1,0:T(8,128)S(1)}, f32[16,2048]{1,0:T(8,128)S(1)}, u32[]{:S(2)}, u32[]{:S(2)}) collective-permute-start(f32[16,2048]{1,0:T(8,128)S(1)} %get-tuple-element.38), channel_id=1, source_target_pairs={{0,3},{1,2},{2,1},{3,0},{4,7},{5,6},{6,5},{7,4},{8,11},{9,10},{10,... | collective-permute-start | bytes 393224 | tf_op jit(solution)/shard_map/ppermute | solution.py:30
where the time goes:
time: 101 us
  Pallas kernels  48.4 us (48%)
  waiting for transfers between devices  26.9 us (27%)
  starting transfers between devices  24.4 us (24%)
    pallas_call x10, Pallas kernels, call(): pl.pallas_call(body, out_shape=tuple(outs), in_specs=[pl.BlockSpec(memory...  48.4 us
    ppermute x18, waiting for transfers between devices, partner(): lax.ppermute(value, 'leaf', [(source, source ^ mask) for source in range(...  26.9 us
    ppermute x18, starting transfers between devices, partner(): lax.ppermute(value, 'leaf', [(source, source ^ mask) for source in range(...  18.9 us
    ppermute x2, starting transfers between devices, staggered(): return lax.ppermute(value, 'leaf', pairs)  5.52 us
  transfers between devices with their start and end apart: 20, of which 5 were waited for; matrix products, arithmetic and copies ran while one was open for 0% of the time, Pallas kernels for 47%

commit v1 on v0

--- a/solution.py
+++ b/solution.py
@@ -134,7 +134,7 @@
 
 def pack_first(
     points, charges, near_list, near_count, gskel, cskel, gbt, cbt,
-    w, w8, x1, urgent, gkeep, ckeep, csend,
+    w, x1, urgent, gkeep, ckeep, csend, c1,
     tile, lists, counts, grow, crow, group, cluster, sems,
 ):
     d = lax.axis_index("leaf")
@@ -160,8 +160,6 @@
             (
                 (points, w.at[pl.ds(0, F)]),
                 (charges, w.at[pl.ds(F, R)]),
-                (points, w8.at[pl.ds(0, F), cols]),
-                (charges, w8.at[pl.ds(F, R), cols]),
                 (points, x1.at[:, cols]),
             )
         )
@@ -184,10 +182,8 @@
             at = start + j * S
             ref[:, at : at + S] = group[16 * j : 16 * j + 16, pl.ds(lane, S)]
     column = jnp.broadcast_to(skeleton_column(crow, 16, tile)[:16, :1], (16, INFO))
-    for half, mask in ((0, 2), (16, 3)):
-        lane = pl.multiple_of((gk ^ mask) * S, S)
-        w8[half : half + 16, PTS : PTS + S] = cluster[:, pl.ds(lane, S)]
-        w8[half : half + 16, PTS + S :] = column
+    cluster_block(c1, 0, cluster, column, gk ^ 2)
+    cluster_block(c1, 16, cluster, column, gk ^ 3)
     cluster_block(ckeep, 0, cluster, column, gk)
     cluster_block(csend, 0, cluster, column, gk ^ 1)
     for copy in large:
@@ -216,7 +212,7 @@
     pay[F:] = product(jnp.concatenate(weights, 1), device[...], NN)
 
 
-def group_up(pay, x1, x1r, urgent, gkeep, ckeep, w8r, c2r, e1, rgbt, skel):
+def group_up(pay, x1, x1r, urgent, gkeep, ckeep, c1r, c2r, e1, rgbt, skel):
     pos = lax.axis_index("leaf") & 3
     sources = (
         (0, gkeep, 0, x1, PTS),
@@ -235,7 +231,7 @@
     e1[F:32, :S] = product(pay[F:], rgbt[...], NT)
     e1[:32, S:] = jnp.zeros((32, INFO), f32)
     e1[32:48] = ckeep[...]
-    e1[48:64] = w8r[:16, PTS:]
+    e1[48:64] = c1r[:16]
     e1[64:96] = c2r[...]
 
 
@@ -302,43 +298,51 @@
     place[4] = 2 - even8
 
     def list_leaf(leaf, filled):
-        def list_slot(slot, filled):
-            source = info[leaf, slot]
-            owner = source >> 2
-            mine = (owner & 3) == pos
-            shard = place[jnp.where(mine, (owner - d + 8) >> 2, 0)]
-            work[filled] = ((shard * 4 + (source & 3)) << 4) | leaf
-            return filled + jnp.where(mine, 1, 0)
-
-        return lax.fori_loop(0, info[leaf, NBR], list_slot, filled)
+        live = info[leaf, NBR]
+
+        def list_slots(step, filled):
+            for u in range(4):
+                slot = step * 4 + u
+                source = info[leaf, slot]
+                owner = source >> 2
+                mine = ((owner & 3) == pos) & (slot < live)
+                shard = place[jnp.where(mine, (owner - d + 8) >> 2, 0)]
+                work[filled] = ((shard * 4 + (source & 3)) << 4) | leaf
+                filled += jnp.where(mine, 1, 0)
+            return filled
+
+        return lax.fori_loop(0, (live + 3) >> 2, list_slots, filled)
 
     return lax.fori_loop(0, 16, list_leaf, 0)
 
 
 def run_tiles(first, last, work, left, right, charge, acc):
-    def tile(n):
-        item = work[n]
-        source = item >> 4
-        target = item & 15
-        values = jnp.exp2(dot(left[source], right[target], NN)).astype(bf16)
-        acc[target] += dot(charge[source], values, NN)
+    def tiles(start, number):
+        items = [work[start + u] for u in range(number)]
+        pairs = [(item >> 4, item & 15) for item in items]
+        exponents = [dot(left[source], right[target], NN) for source, target in pairs]
+        sums = [
+            dot(charge[source], jnp.exp2(exponent).astype(bf16), NN)
+            for (source, _), exponent in zip(pairs, exponents)
+        ]
+        for (_, target), total in zip(pairs, sums):
+            acc[target] += total
 
     def several(step, _):
-        for u in range(UNROLL):
-            tile(first + step * UNROLL + u)
+        tiles(first + step * UNROLL, UNROLL)
         return 0
 
     whole = (last - first) // UNROLL
     lax.fori_loop(0, whole, several, 0)
 
     def single(n, _):
-        tile(n)
+        tiles(n, 1)
         return 0
 
     lax.fori_loop(first + whole * UNROLL, last, single, 0)
 
 
-PARTS = (0, 6, 11, 16)
+PARTS = (0, 5, 9, 13, 16)
 
 
 def bounds(count, part):
@@ -347,19 +351,34 @@
     return first, last if part == len(PARTS) - 2 else last & -UNROLL
 
 
-def near_start(info, w, w8, i8, w4, i4, x1r, targets, acc, left, right, charge, work, place):
+def source_rows(ref, shard, left, charge):
+    for l in range(LEAVES_DEV):
+        cols = slice(l * LEAF, (l + 1) * LEAF)
+        left[4 * shard + l] = jnp.transpose(exponent_rows(ref[:F, cols], True))
+        charge[4 * shard + l] = ref[F:, cols].astype(bf16)
+
+
+def target_rows(ref, at, q, right):
+    for l in range(LEAVES_DEV):
+        right[4 * q + l] = exponent_rows(ref[:F, at + l * LEAF : at + (l + 1) * LEAF], False)
+
+
+def near_plan(info, w, x1r, left, right, charge, work, place):
     count = make_work(info, work, place)
     work[WORK - 1] = count
-    for i, ref in enumerate((w, w8, i8, w4, i4)):
-        for l in range(LEAVES_DEV):
-            cols = slice(l * LEAF, (l + 1) * LEAF)
-            left[4 * i + l] = jnp.transpose(exponent_rows(ref[:F, cols], True))
-            charge[4 * i + l] = ref[F:, cols].astype(bf16)
-    for q, (ref, at) in enumerate(((w, 0), (x1r, 0), (targets, 0), (targets, SPAN))):
-        for l in range(LEAVES_DEV):
-            right[4 * q + l] = exponent_rows(ref[:F, at + l * LEAF : at + (l + 1) * LEAF], False)
+    source_rows(w, 0, left, charge)
+    target_rows(w, 0, 0, right)
+    target_rows(x1r, 0, 1, right)
+
+
+def near_start(work, w8, i8, w4, i4, targets, left0, right0, charge0, acc, left, right, charge):
+    del left0, right0, charge0
+    for i, ref in enumerate((w8, i8, w4, i4)):
+        source_rows(ref, 1 + i, left, charge)
+    for q in range(2):
+        target_rows(targets, q * SPAN, 2 + q, right)
     acc[...] = jnp.zeros_like(acc)
-    run_tiles(*bounds(count, 0), work, left, right, charge, acc)
+    run_tiles(*bounds(work[WORK - 1], 0), work, left, right, charge, acc)
 
 
 def near_more(part):
@@ -395,16 +414,16 @@
     cluster_basis,
     cluster_skeleton,
 ):
-    w, w8, x1, urgent, gkeep, ckeep, csend = call(
+    w, x1, urgent, gkeep, ckeep, csend, c1 = call(
         pack_first,
         (
             out(32, PTS),
-            out(32, PTS + BLOCK),
             out(16, SPAN + 8 * S),
             out(16, 4 * S),
             out(16, 4 * S),
             out(16, BLOCK),
             out(16, BLOCK),
+            out(32, BLOCK),
         ),
         (
             points,
@@ -425,12 +444,13 @@
             pltpu.VMEM((1, 16), jnp.int32),
             pltpu.VMEM((64, 4 * S), f32),
             pltpu.VMEM((16, 4 * S), f32),
-            pltpu.SemaphoreType.DMA((11,)),
+            pltpu.SemaphoreType.DMA((9,)),
         ),
     )
     x1r = partner(x1, 1)
     w4r = partner(w, 4)
-    w8r = partner(w8, 8)
+    c1r = partner(c1, 8)
+    w8r = partner(w, 8)
     i8r = staggered(w, 8)
     i4r = staggered(w, 4)
     urgent = jnp.concatenate([urgent, x1r[:, SPAN + 4 * S :], x1[:, PTS:SPAN], x1r[:, PTS:SPAN]], 1)
@@ -448,11 +468,11 @@
             pltpu.SemaphoreType.DMA((LEAVES_DEV + 1,)),
         ),
     )
-    c2r = partner(jnp.concatenate([csend, w8r[16:, PTS:]], 0), 6)
+    c2r = partner(jnp.concatenate([csend, c1r[16:]], 0), 6)
     e1, rgbt, _ = call(
         group_up,
         (out(96, BLOCK), out(S, S), out(S, 128)),
-        (pay, x1, x1r, urgent, gkeep, ckeep, w8r, c2r),
+        (pay, x1, x1r, urgent, gkeep, ckeep, c1r, c2r),
     )
     g1, g2, g3 = (partner(e1, m) for m in (1, 2, 3))
     e2, rcbt, _ = call(cluster_up, (out(32, 2 * S), out(S, S), out(S, 128)), (e1, g1, g2, g3))
@@ -468,24 +488,30 @@
         [
             x1[:4, PTS:SPAN],
             x1r[:4, PTS:SPAN],
-            targets[:4, PTS:SPAN],
-            targets[:4, SPAN + PTS :],
+            urgent[:4, 8 * S : 8 * S + INFO],
+            urgent[:4, 8 * S + INFO :],
         ],
         0,
     ).astype(jnp.int32)
-    acc, left, right, charge, work = call(
+    rows = (
+        jax.ShapeDtypeStruct((20, LEAF, 128), bf16),
+        jax.ShapeDtypeStruct((16, 128, LEAF), bf16),
+        jax.ShapeDtypeStruct((20, R, LEAF), bf16),
+    )
+    left, right, charge, work = call(
+        near_plan,
+        (*rows, jax.ShapeDtypeStruct((WORK,), jnp.int32)),
+        (info, w, x1r),
+        smem=(0,),
+        smem_outs=(3,),
+        scratch=(pltpu.SMEM((8,), jnp.int32),),
+    )
+    acc, left, right, charge = call(
         near_start,
-        (
-            out(16, R, LEAF),
-            jax.ShapeDtypeStruct((20, LEAF, 128), bf16),
-            jax.ShapeDtypeStruct((16, 128, LEAF), bf16),
-            jax.ShapeDtypeStruct((20, R, LEAF), bf16),
-            jax.ShapeDtypeStruct((WORK,), jnp.int32),
-        ),
-        (info, w, w8r, i8r, w4r, i4r, x1r, targets),
+        (out(16, R, LEAF), *rows),
+        (work, w8r, i8r, w4r, i4r, targets, left, right, charge),
         smem=(0,),
-        smem_outs=(4,),
-        scratch=(pltpu.SMEM((8,), jnp.int32),),
+        aliases={6: 1, 7: 2, 8: 3},
     )
     for part in range(1, len(PARTS) - 2):
         (acc,) = call(

time: 101 us -> 89.3 us (0.88)
  Pallas kernels: 48.4 us -> 39.3 us
  waiting for transfers between devices: 26.9 us -> 24.3 us
    pallas_call x10 -> x12, Pallas kernels: 48.4 us -> 39.3 us  [call(): pl.pallas_call(body, out_shape=tuple(outs), in_specs=[pl.BlockSpec(memory...]
    ppermute x18 -> x19, waiting for transfers between devices: 26.9 us -> 24.3 us  [partner(): lax.ppermute(value, 'leaf', [(source, source ^ mask) for source in range(...]
    ppermute x18 -> x19, starting transfers between devices: 18.9 us -> 17.9 us  [partner(): lax.ppermute(value, 'leaf', [(source, source ^ mask) for source in range(...]
  transfers between devices with their start and end apart: 20 -> 21, of which waited for: 5 -> 6; matrix products, arithmetic and copies ran while one was open for 0% -> 0% of each run, Pallas kernels for 47% -> 41%
where the time goes in v1:
time: 89.3 us; the launch traced here: 89.2 us
  Pallas kernels  39.3 us (44%)
  waiting for transfers between devices  24.3 us (27%)
  starting transfers between devices  23.8 us (27%)
    pallas_call x12, Pallas kernels, call(): pl.pallas_call(body, out_shape=tuple(outs), in_specs=[pl.BlockSpec(memory...  39.3 us
    ppermute x19, waiting for transfers between devices, partner(): lax.ppermute(value, 'leaf', [(source, source ^ mask) for source in range(...  24.3 us
    ppermute x19, starting transfers between devices, partner(): lax.ppermute(value, 'leaf', [(source, source ^ mask) for source in range(...  17.9 us
    ppermute x2, starting transfers between devices, staggered(): return lax.ppermute(value, 'leaf', pairs)  5.98 us
  transfers between devices with their start and end apart: 21, of which 6 were waited for; matrix products, arithmetic and copies ran while one was open for 0% of the time, Pallas kernels for 41%

profile of v1, /device:TPU:9, one launch (start us, length us, event | category | flops | bytes accessed | tf_op | source)
XLA Modules:
  0.0 89.2 jit_solution(245148546418353415)
XLA Ops:
  0.0 1.3 %shard_map.109 = (f32[32,2048]{1,0:T(8,128)S(1)}, f32[16,4224]{1,0:T(8,128)S(1)}, f32[16,1024]{1,0:T(8,128)S(1)}, f32[16,1024]{1,0:T(8,128)S(1)}, f32[16,384]{1,...) custom-call(f32[16,2048]{1,0:T(8,128)} %points.1, f32[16,2048]{1,0:T(8,128)} %charges.1, s32[4,32]{1,0:T(4,128)} %near_list.1, ...), custom_call_target="tpu_custom_call" | custom-call | tf_op jit(solution)/shard_map/pallas_call | solution.py:51
  2.0 1.6 %collective-permute-start.10 = (f32[32,384]{1,0:T(8,128)S(1)}, f32[32,384]{1,0:T(8,128)S(1)}, u32[]{:S(2)}, u32[]{:S(2)}) collective-permute-start(f32[32,384]{1,0:T(8,128)S(1)} %get-tuple-element.47), channel_id=1, source_target_pairs={{0,8},{1,9},{2,10},{3,11},{4,12},{5,13},{6,14},{7,15},{8,0},{9,1},... | collective-permute-start | bytes 147464 | tf_op jit(solution)/shard_map/ppermute | solution.py:30
  3.7 1.9 %collective-permute-done.10.c1r = f32[32,384]{1,0:T(8,128)S(1)} collective-permute-done((f32[32,384]{1,0:T(8,128)S(1)}, f32[32,384]{1,0:T(8,128)S(1)}, u32[]{:S(2)}, u32[]{:S(2)}) %collective-permute-start.10) | collective-permute-done | bytes 49184 | tf_op jit(solution)/shard_map/ppermute | solution.py:30
  5.6 1.3 %collective-permute-start.1 = (f32[16,2304]{1,0:T(8,128)S(1)}, f32[16,2304]{1,0:T(8,128)S(1)}, u32[]{:S(2)}, u32[]{:S(2)}) collective-permute-start(f32[16,2304]{1,0:T(8,128)S(1)} %pad_maximum_fusion.1), channel_id=1, source_target_pairs={{0,2},{1,3},{2,0},{3,1},{4,6},{5,7},{6,4},{7,5},{8,10},{9,11},{10,... | collective-permute-start | bytes 442376 | tf_op jit(solution)/shard_map/ppermute | solution.py:30
  6.9 1.8 %collective-permute-start.11 = (f32[32,384]{1,0:T(8,128)S(1)}, f32[32,384]{1,0:T(8,128)S(1)}, u32[]{:S(2)}, u32[]{:S(2)}) collective-permute-start(f32[32,384]{1,0:T(8,128)S(1)} %pad_maximum_fusion.4), channel_id=1, source_target_pairs={{0,6},{1,7},{2,4},{3,5},{4,2},{5,3},{6,0},{7,1},{8,14},{9,15},{10,... | collective-permute-start | bytes 147464 | tf_op jit(solution)/shard_map/ppermute | solution.py:30
  9.4 2.5 %shard_map.115.pay = f32[32,256]{1,0:T(8,128)S(1)} custom-call(f32[32,2048]{1,0:T(8,128)S(1)} %get-tuple-element.32.w, f32[2048,256]{1,0:T(8,128)} %leaf.1, f32[1024,256]{1,0:T(8,128)} %device.1, s32[1,256]{1,0:T(1,128)S(1)} %copy-done.2), custom_call_target="tpu_custom_call" | custom-call | tf_op jit(solution)/shard_map/pallas_call | solution.py:51
  12.7 1.5 %collective-permute-start.14 = (f32[96,384]{1,0:T(8,128)S(1)}, f32[96,384]{1,0:T(8,128)S(1)}, u32[]{:S(2)}, u32[]{:S(2)}) collective-permute-start(f32[96,384]{1,0:T(8,128)S(1)} %get-tuple-element.49.e1), channel_id=1, source_target_pairs={{0,3},{1,2},{2,1},{3,0},{4,7},{5,6},{6,5},{7,4},{8,11},{9,10},{10,... | collective-permute-start | bytes 442376 | tf_op jit(solution)/shard_map/ppermute | solution.py:30
  15.4 3.1 %collective-permute-done.14.r3 = f32[96,384]{1,0:T(8,128)S(1)} collective-permute-done((f32[96,384]{1,0:T(8,128)S(1)}, f32[96,384]{1,0:T(8,128)S(1)}, u32[]{:S(2)}, u32[]{:S(2)}) %collective-permute-start.14) | collective-permute-done | bytes 147488 | tf_op jit(solution)/shard_map/ppermute | solution.py:30
  18.5 3.5 %collective-permute-done.13.r2 = f32[96,384]{1,0:T(8,128)S(1)} collective-permute-done((f32[96,384]{1,0:T(8,128)S(1)}, f32[96,384]{1,0:T(8,128)S(1)}, u32[]{:S(2)}, u32[]{:S(2)}) %collective-permute-start.13) | collective-permute-done | bytes 147488 | tf_op jit(solution)/shard_map/ppermute | solution.py:30
  22.7 2.2 %collective-permute-start.17 = (f32[32,512]{1,0:T(8,128)S(1)}, f32[32,512]{1,0:T(8,128)S(1)}, u32[]{:S(2)}, u32[]{:S(2)}) collective-permute-start(f32[32,512]{1,0:T(8,128)S(1)} %get-tuple-element.50.e2), channel_id=1, source_target_pairs={{0,14},{1,15},{2,12},{3,13},{4,10},{5,11},{6,8},{7,9},{8,6},{9,7},... | collective-permute-start | bytes 196616 | tf_op jit(solution)/shard_map/ppermute | solution.py:30
  24.9 1.5 %collective-permute-start.16 = (f32[32,512]{1,0:T(8,128)S(1)}, f32[32,512]{1,0:T(8,128)S(1)}, u32[]{:S(2)}, u32[]{:S(2)}) collective-permute-start(f32[32,512]{1,0:T(8,128)S(1)} %get-tuple-element.50.e2), channel_id=1, source_target_pairs={{0,6},{1,7},{2,4},{3,5},{4,2},{5,3},{6,0},{7,1},{8,14},{9,15},{10,... | collective-permute-start | bytes 196616 | tf_op jit(solution)/shard_map/ppermute | solution.py:30
  26.6 3.6 %collective-permute-start.5 = (f32[32,2048]{1,0:T(8,128)S(1)}, f32[32,2048]{1,0:T(8,128)S(1)}, u32[]{:S(2)}, u32[]{:S(2)}) collective-permute-start(f32[32,2048]{1,0:T(8,128)S(1)} %get-tuple-element.32.w), channel_id=1, source_target_pairs={{0,124},{1,125},{2,126},{3,127},{4,8},{5,9},{6,10},{7,11},{8,4},{9... | collective-permute-start | bytes 786440 | tf_op jit(solution)/shard_map/ppermute | solution.py:39
  30.6 2.4 %collective-permute-start.3 = (f32[32,2048]{1,0:T(8,128)S(1)}, f32[32,2048]{1,0:T(8,128)S(1)}, u32[]{:S(2)}, u32[]{:S(2)}) collective-permute-start(f32[32,2048]{1,0:T(8,128)S(1)} %get-tuple-element.32.w), channel_id=1, source_target_pairs={{0,120},{1,121},{2,122},{3,123},{4,124},{5,125},{6,126},{7,127},{8... | collective-permute-start | bytes 786440 | tf_op jit(solution)/shard_map/ppermute | solution.py:39
  34.5 11.1 %collective-permute-done.18.c1 = f32[32,256]{1,0:T(8,128)S(1)} collective-permute-done((f32[32,256]{1,0:T(8,128)S(1)}, f32[32,256]{1,0:T(8,128)S(1)}, u32[]{:S(2)}, u32[]{:S(2)}) %collective-permute-start.18) | collective-permute-done | bytes 32800 | tf_op jit(solution)/shard_map/ppermute | solution.py:30
  45.7 1.5 %collective-permute-start.19 = (f32[32,512]{1,0:T(8,128)S(1)}, f32[32,512]{1,0:T(8,128)S(1)}, u32[]{:S(2)}, u32[]{:S(2)}) collective-permute-start(f32[32,512]{1,0:T(8,128)S(1)} %pad_maximum_fusion.3), channel_id=1, source_target_pairs={{0,32},{1,33},{2,34},{3,35},{4,36},{5,37},{6,38},{7,39},{8,40},{9,... | collective-permute-start | bytes 196616 | tf_op jit(solution)/shard_map/ppermute | solution.py:30
  47.1 4.5 %shard_map.110 = (bf16[20,512,128]{2,1,0:T(8,128)(2,1)S(1)}, bf16[16,128,512]{2,1,0:T(8,128)(2,1)S(1)}, bf16[20,16,512]{2,1,0:T(8,128)(2,1)S(1)}, s32[528]{0:T(1024)S(1)}) custom-call(s32[16,128]{1,0:T(8,128)S(1)} %maximum_convert_fusion.info, f32[32,2048]{1,0:T(8,128)S(1)} %get-tuple-element.32.w, f32[16,4224]{1,0:T(8,128)S(1)} %collective-permute-done.x1r), custom_call_target="tpu_custom_call" | custom-call | tf_op jit(solution)/shard_map/pallas_call | solution.py:51
  51.6 1.7 %collective-permute-done.6.targets = f32[16,4352]{1,0:T(8,128)S(1)} collective-permute-done((f32[16,4352]{1,0:T(8,128)S(1)}, f32[16,4352]{1,0:T(8,128)S(1)}, u32[]{:S(2)}, u32[]{:S(2)}) %collective-permute-start.6) | collective-permute-done | bytes 278560 | tf_op jit(solution)/shard_map/ppermute | solution.py:30
  53.4 7.9 %shard_map.111 = (f32[16,16,512]{2,1,0:T(8,128)S(1)}, bf16[20,512,128]{2,1,0:T(8,128)(2,1)S(1)}, bf16[16,128,512]{2,1,0:T(8,128)(2,1)S(1)}, bf16[20,16,512]{2,1,0:T(8,128)(2,1)S(1)}) custom-call(s32[528]{0:T(1024)S(1)} %get-tuple-element.33.work, ...), custom_call_target="tpu_custom_call", output_to_operand_aliasing={{1}: (6, {}), {2}: (7, {}), {3}: (8, {})} | custom-call | tf_op jit(solution)/shard_map/pallas_call | solution.py:51
  61.3 7.1 %shard_map.112.before = f32[16,16,512]{2,1,0:T(8,128)S(1)} custom-call(s32[528]{0:T(1024)S(1)} %get-tuple-element.33.work, bf16[20,512,128]{2,1,0:T(8,128)(2,1)S(1)} %get-tuple-element.37.left, bf16[16,128,512]{2,1,0:T(8,128)(2,1)S(1)} %get-tuple-element.38.right, bf16[20,16,512]{2,1,0:T(8,128)(2,1)S(1)} %get-tuple-element.39.charge, ...), custom_call_target="tpu_custom_call", output_to_operand_aliasing={{}: (4, {})} | custom-call | tf_op jit(solution)/shard_map/pallas_call | solution.py:51
  68.5 6.2 %shard_map.113.before = f32[16,16,512]{2,1,0:T(8,128)S(1)} custom-call(s32[528]{0:T(1024)S(1)} %get-tuple-element.33.work, bf16[20,512,128]{2,1,0:T(8,128)(2,1)S(1)} %get-tuple-element.37.left, bf16[16,128,512]{2,1,0:T(8,128)(2,1)S(1)} %get-tuple-element.38.right, bf16[20,16,512]{2,1,0:T(8,128)(2,1)S(1)} %get-tuple-element.39.charge, ...), custom_call_target="tpu_custom_call", output_to_operand_aliasing={{}: (4, {})} | custom-call | tf_op jit(solution)/shard_map/pallas_call | solution.py:51
  74.7 5.3 %shard_map.114 = (f32[16,2048]{1,0:T(8,128)S(1)}, f32[16,2048]{1,0:T(8,128)S(1)}, f32[16,2048]{1,0:T(8,128)S(1)}, f32[16,2048]{1,0:T(8,128)S(1)}) custom-call(s32[528]{0:T(1024)S(1)} %get-tuple-element.33.work, bf16[20,512,128]{2,1,0:T(8,128)(2,1)S(1)} %get-tuple-element.37.left, bf16[16,128,512]{2,1,0:T(8,128)(2,1)S(1)} %get-tuple-element.38.right, ...), custom_call_target="tpu_custom_call" | custom-call | tf_op jit(solution)/shard_map/pallas_call | solution.py:51
  80.4 2.0 %collective-permute-start.9 = (f32[16,2048]{1,0:T(8,128)S(1)}, f32[16,2048]{1,0:T(8,128)S(1)}, u32[]{:S(2)}, u32[]{:S(2)}) collective-permute-start(f32[16,2048]{1,0:T(8,128)S(1)} %get-tuple-element.44), channel_id=1, source_target_pairs={{0,3},{1,2},{2,1},{3,0},{4,7},{5,6},{6,5},{7,4},{8,11},{9,10},{10,... | collective-permute-start | bytes 393224 | tf_op jit(solution)/shard_map/ppermute | solution.py:30
  83.2 2.3 %shard_map.120 = f32[16,2048]{1,0:T(8,128)S(1)} custom-call(f32[32,256]{1,0:T(8,128)S(1)} %shard_map.118.cpay, f32[32,1024]{1,0:T(8,128)S(1)} %collective-permute-done.20.c3, f32[16,256]{1,0:T(8,128)S(1)} %get-tuple-element.51.side, f32[16,256]{1,0:T(8,128)S(1)} %get-tuple-element.52.top, f32[256,256]{1,0:T(8,128)S(1)} %get-tuple-element.53.rcbt, ...), custom_call_target="tpu_custom_call" | custom-call | tf_op jit(solution)/shard_map/pallas_call | solution.py:51
  85.5 2.9 %collective-permute-done.9 = f32[16,2048]{1,0:T(8,128)S(1)} collective-permute-done((f32[16,2048]{1,0:T(8,128)S(1)}, f32[16,2048]{1,0:T(8,128)S(1)}, u32[]{:S(2)}, u32[]{:S(2)}) %collective-permute-start.9) | collective-permute-done | bytes 131104 | tf_op jit(solution)/shard_map/ppermute | solution.py:30
  (52 shorter events, 8.2 us)
Async XLA Ops:
  1.3 4.3 %collective-permute-start = (f32[16,4224]{1,0:T(8,128)S(1)}, f32[16,4224]{1,0:T(8,128)S(1)}, u32[]{:S(2)}, u32[]{:S(2)}) collective-permute-start(f32[16,4224]{1,0:T(8,128)S(1)} %get-tuple-element.30.x1), channel_id=1, source_target_pairs={{0,1},{1,0},{2,3},{3,2},{4,5},{5,4},{6,7},{7,6},{8,9},{9,8},{10,11... | collective-permute-start | bytes 811016 | tf_op jit(solution)/shard_map/ppermute | solution.py:30
  2.0 3.6 %collective-permute-start.10 = (f32[32,384]{1,0:T(8,128)S(1)}, f32[32,384]{1,0:T(8,128)S(1)}, u32[]{:S(2)}, u32[]{:S(2)}) collective-permute-start(f32[32,384]{1,0:T(8,128)S(1)} %get-tuple-element.47), channel_id=1, source_target_pairs={{0,8},{1,9},{2,10},{3,11},{4,12},{5,13},{6,14},{7,15},{8,0},{9,1},... | collective-permute-start | bytes 147464 | tf_op jit(solution)/shard_map/ppermute | solution.py:30
  5.6 6.3 %collective-permute-start.1 = (f32[16,2304]{1,0:T(8,128)S(1)}, f32[16,2304]{1,0:T(8,128)S(1)}, u32[]{:S(2)}, u32[]{:S(2)}) collective-permute-start(f32[16,2304]{1,0:T(8,128)S(1)} %pad_maximum_fusion.1), channel_id=1, source_target_pairs={{0,2},{1,3},{2,0},{3,1},{4,6},{5,7},{6,4},{7,5},{8,10},{9,11},{10,... | collective-permute-start | bytes 442376 | tf_op jit(solution)/shard_map/ppermute | solution.py:30
  6.9 5.0 %collective-permute-start.11 = (f32[32,384]{1,0:T(8,128)S(1)}, f32[32,384]{1,0:T(8,128)S(1)}, u32[]{:S(2)}, u32[]{:S(2)}) collective-permute-start(f32[32,384]{1,0:T(8,128)S(1)} %pad_maximum_fusion.4), channel_id=1, source_target_pairs={{0,6},{1,7},{2,4},{3,5},{4,2},{5,3},{6,0},{7,1},{8,14},{9,15},{10,... | collective-permute-start | bytes 147464 | tf_op jit(solution)/shard_map/ppermute | solution.py:30
  8.7 0.7 copy-start.2
  12.7 5.8 %collective-permute-start.14 = (f32[96,384]{1,0:T(8,128)S(1)}, f32[96,384]{1,0:T(8,128)S(1)}, u32[]{:S(2)}, u32[]{:S(2)}) collective-permute-start(f32[96,384]{1,0:T(8,128)S(1)} %get-tuple-element.49.e1), channel_id=1, source_target_pairs={{0,3},{1,2},{2,1},{3,0},{4,7},{5,6},{6,5},{7,4},{8,11},{9,10},{10,... | collective-permute-start | bytes 442376 | tf_op jit(solution)/shard_map/ppermute | solution.py:30
  14.2 7.8 %collective-permute-start.13 = (f32[96,384]{1,0:T(8,128)S(1)}, f32[96,384]{1,0:T(8,128)S(1)}, u32[]{:S(2)}, u32[]{:S(2)}) collective-permute-start(f32[96,384]{1,0:T(8,128)S(1)} %get-tuple-element.49.e1), channel_id=1, source_target_pairs={{0,2},{1,3},{2,0},{3,1},{4,6},{5,7},{6,4},{7,5},{8,10},{9,11},{10,... | collective-permute-start | bytes 442376 | tf_op jit(solution)/shard_map/ppermute | solution.py:30
  15.4 6.6 %collective-permute-start.12 = (f32[96,384]{1,0:T(8,128)S(1)}, f32[96,384]{1,0:T(8,128)S(1)}, u32[]{:S(2)}, u32[]{:S(2)}) collective-permute-start(f32[96,384]{1,0:T(8,128)S(1)} %get-tuple-element.49.e1), channel_id=1, source_target_pairs={{0,1},{1,0},{2,3},{3,2},{4,5},{5,4},{6,7},{7,6},{8,9},{9,8},{10,11... | collective-permute-start | bytes 442376 | tf_op jit(solution)/shard_map/ppermute | solution.py:30
  22.7 7.9 %collective-permute-start.17 = (f32[32,512]{1,0:T(8,128)S(1)}, f32[32,512]{1,0:T(8,128)S(1)}, u32[]{:S(2)}, u32[]{:S(2)}) collective-permute-start(f32[32,512]{1,0:T(8,128)S(1)} %get-tuple-element.50.e2), channel_id=1, source_target_pairs={{0,14},{1,15},{2,12},{3,13},{4,10},{5,11},{6,8},{7,9},{8,6},{9,7},... | collective-permute-start | bytes 196616 | tf_op jit(solution)/shard_map/ppermute | solution.py:30
  24.9 8.0 %collective-permute-start.16 = (f32[32,512]{1,0:T(8,128)S(1)}, f32[32,512]{1,0:T(8,128)S(1)}, u32[]{:S(2)}, u32[]{:S(2)}) collective-permute-start(f32[32,512]{1,0:T(8,128)S(1)} %get-tuple-element.50.e2), channel_id=1, source_target_pairs={{0,6},{1,7},{2,4},{3,5},{4,2},{5,3},{6,0},{7,1},{8,14},{9,15},{10,... | collective-permute-start | bytes 196616 | tf_op jit(solution)/shard_map/ppermute | solution.py:30
  26.4 7.3 %collective-permute-start.15 = (f32[32,512]{1,0:T(8,128)S(1)}, f32[32,512]{1,0:T(8,128)S(1)}, u32[]{:S(2)}, u32[]{:S(2)}) collective-permute-start(f32[32,512]{1,0:T(8,128)S(1)} %get-tuple-element.50.e2), channel_id=1, source_target_pairs={{0,8},{1,9},{2,10},{3,11},{4,12},{5,13},{6,14},{7,15},{8,0},{9,1},... | collective-permute-start | bytes 196616 | tf_op jit(solution)/shard_map/ppermute | solution.py:30
  26.6 19.1 %collective-permute-start.5 = (f32[32,2048]{1,0:T(8,128)S(1)}, f32[32,2048]{1,0:T(8,128)S(1)}, u32[]{:S(2)}, u32[]{:S(2)}) collective-permute-start(f32[32,2048]{1,0:T(8,128)S(1)} %get-tuple-element.32.w), channel_id=1, source_target_pairs={{0,124},{1,125},{2,126},{3,127},{4,8},{5,9},{6,10},{7,11},{8,4},{9... | collective-permute-start | bytes 786440 | tf_op jit(solution)/shard_map/ppermute | solution.py:39
  30.2 21.4 %collective-permute-start.4 = (f32[32,2048]{1,0:T(8,128)S(1)}, f32[32,2048]{1,0:T(8,128)S(1)}, u32[]{:S(2)}, u32[]{:S(2)}) collective-permute-start(f32[32,2048]{1,0:T(8,128)S(1)} %get-tuple-element.32.w), channel_id=1, source_target_pairs={{0,4},{1,5},{2,6},{3,7},{4,0},{5,1},{6,2},{7,3},{8,12},{9,13},{10,... | collective-permute-start | bytes 786440 | tf_op jit(solution)/shard_map/ppermute | solution.py:30
  30.6 21.0 %collective-permute-start.3 = (f32[32,2048]{1,0:T(8,128)S(1)}, f32[32,2048]{1,0:T(8,128)S(1)}, u32[]{:S(2)}, u32[]{:S(2)}) collective-permute-start(f32[32,2048]{1,0:T(8,128)S(1)} %get-tuple-element.32.w), channel_id=1, source_target_pairs={{0,120},{1,121},{2,122},{3,123},{4,124},{5,125},{6,126},{7,127},{8... | collective-permute-start | bytes 786440 | tf_op jit(solution)/shard_map/ppermute | solution.py:39
  33.0 18.7 %collective-permute-start.2 = (f32[32,2048]{1,0:T(8,128)S(1)}, f32[32,2048]{1,0:T(8,128)S(1)}, u32[]{:S(2)}, u32[]{:S(2)}) collective-permute-start(f32[32,2048]{1,0:T(8,128)S(1)} %get-tuple-element.32.w), channel_id=1, source_target_pairs={{0,8},{1,9},{2,10},{3,11},{4,12},{5,13},{6,14},{7,15},{8,0},{9,1},... | collective-permute-start | bytes 786440 | tf_op jit(solution)/shard_map/ppermute | solution.py:30
  33.7 12.0 %collective-permute-start.18 = (f32[32,256]{1,0:T(8,128)S(1)}, f32[32,256]{1,0:T(8,128)S(1)}, u32[]{:S(2)}, u32[]{:S(2)}) collective-permute-start(f32[32,256]{1,0:T(8,128)S(1)} %shard_map.118.cpay), channel_id=1, source_target_pairs={{0,24},{1,25},{2,26},{3,27},{4,28},{5,29},{6,30},{7,31},{8,16},{9,... | collective-permute-start | bytes 98312 | tf_op jit(solution)/shard_map/ppermute | solution.py:30
  45.6 7.7 %collective-permute-start.6 = (f32[16,4352]{1,0:T(8,128)S(1)}, f32[16,4352]{1,0:T(8,128)S(1)}, u32[]{:S(2)}, u32[]{:S(2)}) collective-permute-start(f32[16,4352]{1,0:T(8,128)S(1)} %pad_maximum_fusion), channel_id=1, source_target_pairs={{0,2},{1,3},{2,0},{3,1},{4,6},{5,7},{6,4},{7,5},{8,10},{9,11},{10,... | collective-permute-start | bytes 835592 | tf_op jit(solution)/shard_map/ppermute | solution.py:30
  45.7 22.8 %collective-permute-start.19 = (f32[32,512]{1,0:T(8,128)S(1)}, f32[32,512]{1,0:T(8,128)S(1)}, u32[]{:S(2)}, u32[]{:S(2)}) collective-permute-start(f32[32,512]{1,0:T(8,128)S(1)} %pad_maximum_fusion.3), channel_id=1, source_target_pairs={{0,32},{1,33},{2,34},{3,35},{4,36},{5,37},{6,38},{7,39},{8,40},{9,... | collective-permute-start | bytes 196616 | tf_op jit(solution)/shard_map/ppermute | solution.py:30
  68.5 14.8 %collective-permute-start.20 = (f32[32,1024]{1,0:T(8,128)S(1)}, f32[32,1024]{1,0:T(8,128)S(1)}, u32[]{:S(2)}, u32[]{:S(2)}) collective-permute-start(f32[32,1024]{1,0:T(8,128)S(1)} %pad_maximum_fusion.2), channel_id=1, source_target_pairs={{0,96},{1,97},{2,98},{3,99},{4,100},{5,101},{6,102},{7,103},{8,104... | collective-permute-start | bytes 393224 | tf_op jit(solution)/shard_map/ppermute | solution.py:30
  74.7 8.5 %copy-start = (f32[2048,256]{1,0:T(8,128)S(1)}, f32[2048,256]{1,0:T(8,128)}, u32[]{:S(2)}) copy-start(f32[2048,256]{1,0:T(8,128)} %leaf.1) | copy-start | bytes 6291460
  74.7 8.5 %copy-start.1 = (f32[1024,256]{1,0:T(8,128)S(1)}, f32[1024,256]{1,0:T(8,128)}, u32[]{:S(2)}) copy-start(f32[1024,256]{1,0:T(8,128)} %device.1) | copy-start | bytes 3145732
  80.1 5.5 %collective-permute-start.7 = (f32[16,2048]{1,0:T(8,128)S(1)}, f32[16,2048]{1,0:T(8,128)S(1)}, u32[]{:S(2)}, u32[]{:S(2)}) collective-permute-start(f32[16,2048]{1,0:T(8,128)S(1)} %get-tuple-element.42), channel_id=1, source_target_pairs={{0,1},{1,0},{2,3},{3,2},{4,5},{5,4},{6,7},{7,6},{8,9},{9,8},{10,11... | collective-permute-start | bytes 393224 | tf_op jit(solution)/shard_map/ppermute | solution.py:30
  80.4 5.2 %collective-permute-start.8 = (f32[16,2048]{1,0:T(8,128)S(1)}, f32[16,2048]{1,0:T(8,128)S(1)}, u32[]{:S(2)}, u32[]{:S(2)}) collective-permute-start(f32[16,2048]{1,0:T(8,128)S(1)} %get-tuple-element.43), channel_id=1, source_target_pairs={{0,2},{1,3},{2,0},{3,1},{4,6},{5,7},{6,4},{7,5},{8,10},{9,11},{10,... | collective-permute-start | bytes 393224 | tf_op jit(solution)/shard_map/ppermute | solution.py:30
  80.4 8.0 %collective-permute-start.9 = (f32[16,2048]{1,0:T(8,128)S(1)}, f32[16,2048]{1,0:T(8,128)S(1)}, u32[]{:S(2)}, u32[]{:S(2)}) collective-permute-start(f32[16,2048]{1,0:T(8,128)S(1)} %get-tuple-element.44), channel_id=1, source_target_pairs={{0,3},{1,2},{2,1},{3,0},{4,7},{5,6},{6,5},{7,4},{8,11},{9,10},{10,... | collective-permute-start | bytes 393224 | tf_op jit(solution)/shard_map/ppermute | solution.py:30

commit v2 on v1

--- a/solution.py
+++ b/solution.py
@@ -33,8 +33,10 @@
 def staggered(value, step):
     size = lax.axis_size("leaf")
     pairs = [
-        (source, (source + (step if source // step % 2 else -step)) % size)
-        for source in range(size)
+        (source, target if 0 <= target < size else source)
+        for source, target in (
+            (source, source + (step if source // step % 2 else -step)) for source in range(size)
+        )
     ]
     return lax.ppermute(value, "leaf", pairs)
 
@@ -121,11 +123,6 @@
 BLOCK = S + INFO
 
 
-def cluster_block(ref, row, cbt, cskel, gk):
-    ref[row : row + 16, :S] = cbt[:, pl.ds(pl.multiple_of(gk * S, S), S)]
-    ref[row : row + 16, S:] = cskel
-
-
 def skeleton_column(row_ref, count, tile):
     tile[...] = jnp.zeros((8, 128), f32)
     tile[0:1, :count] = row_ref[:, :count].astype(f32)
@@ -134,7 +131,7 @@
 
 def pack_first(
     points, charges, near_list, near_count, gskel, cskel, gbt, cbt,
-    w, x1, urgent, gkeep, ckeep, csend, c1,
+    w, x2, gnext, gkeep, ckeep, c8, c6, c14,
     tile, lists, counts, grow, crow, group, cluster, sems,
 ):
     d = lax.axis_index("leaf")
@@ -160,45 +157,47 @@
             (
                 (points, w.at[pl.ds(0, F)]),
                 (charges, w.at[pl.ds(F, R)]),
-                (points, x1.at[:, cols]),
+                (points, x2.at[:, cols]),
             )
         )
     ]
     for copy in small + large:
         copy.start()
-    x1[:, PTS:SPAN] = jnp.zeros((F, INFO), f32)
+    x2[:, PTS:SPAN] = jnp.zeros((F, INFO), f32)
     for copy in small:
         copy.wait()
-    x1[:4, PTS : PTS + NBR] = lists[...].astype(f32)
+    x2[:4, PTS : PTS + NBR] = lists[...].astype(f32)
     for l in range(LEAVES_DEV):
-        x1[l : l + 1, PTS + NBR : PTS + NBR + 1] = jnp.full((1, 1), counts[l], jnp.int32).astype(f32)
+        x2[l : l + 1, PTS + NBR : PTS + NBR + 1] = jnp.full((1, 1), counts[l], jnp.int32).astype(f32)
     column = skeleton_column(grow, 64, tile)
     for j in range(4):
         lane = PTS + SKEL_LANE + j
-        x1[:, lane : lane + 1] = column[16 * j : 16 * j + 16, :1]
-    for ref, start, mask in ((x1, SPAN, 1), (x1, SPAN + 4 * S, 3), (gkeep, 0, 0), (urgent, 0, 2)):
+        x2[:, lane : lane + 1] = column[16 * j : 16 * j + 16, :1]
+    for ref, start, mask in ((x2, SPAN, 2), (x2, SPAN + 4 * S, 3), (gkeep, 0, 0), (gnext, 0, 1)):
         lane = pl.multiple_of((pos ^ mask) * S, S)
         for j in range(4):
             at = start + j * S
             ref[:, at : at + S] = group[16 * j : 16 * j + 16, pl.ds(lane, S)]
     column = jnp.broadcast_to(skeleton_column(crow, 16, tile)[:16, :1], (16, INFO))
-    cluster_block(c1, 0, cluster, column, gk ^ 2)
-    cluster_block(c1, 16, cluster, column, gk ^ 3)
-    cluster_block(ckeep, 0, cluster, column, gk)
-    cluster_block(csend, 0, cluster, column, gk ^ 1)
+    for ref, mask in ((ckeep, 0), (c8, 2), (c6, 1), (c14, 3)):
+        ref[:, :S] = cluster[:, pl.ds(pl.multiple_of((gk ^ mask) * S, S), S)]
+        ref[:, S:] = column
     for copy in large:
         copy.wait()
 
 
-def device_up(w, leaf_hbm, device_hbm, skeleton, pay, leaf, device, sems):
+def device_up(w, leaf_hbm, device_hbm, skeleton_hbm, pay, leaf, device, skeleton, sems):
     copies = []
     for l in range(LEAVES_DEV):
         rows = pl.ds(l * LEAF, LEAF)
         copies.append(pltpu.make_async_copy(leaf_hbm.at[rows], leaf.at[rows], sems.at[l]))
     last = pltpu.make_async_copy(device_hbm, device, sems.at[LEAVES_DEV])
+    index = pltpu.make_async_copy(skeleton_hbm, skeleton, sems.at[LEAVES_DEV + 1])
+    index.start()
     for copy in copies:
         copy.start()
     last.start()
+    index.wait()
     rows = lax.broadcasted_iota(jnp.int32, (PTS, S), 0)
     one_hot = jnp.where(rows == skeleton[...], 1.0, 0.0).astype(bf16)
     pay[:F] = pick(w[:F], one_hot, NN)
@@ -212,13 +211,13 @@
     pay[F:] = product(jnp.concatenate(weights, 1), device[...], NN)
 
 
-def group_up(pay, x1, x1r, urgent, gkeep, ckeep, c1r, c2r, e1, rgbt, skel):
+def group_up(pay, x2, x2r, x1r, gkeep, ckeep, c8, c6, c14, e1, rgbt, skel):
     pos = lax.axis_index("leaf") & 3
     sources = (
-        (0, gkeep, 0, x1, PTS),
-        (1, x1r, SPAN, x1r, PTS),
-        (2, urgent, 0, urgent, 8 * S),
-        (3, urgent, 4 * S, urgent, 8 * S + INFO),
+        (0, gkeep, 0, x2, PTS),
+        (1, x1r, 2 * SPAN, x1r, PTS),
+        (2, x2r, SPAN, x2r, PTS),
+        (3, x1r, 2 * SPAN + 4 * S, x1r, SPAN + PTS),
     )
     for mask, ref, at, info, info_at in sources:
         first = (pos ^ mask) * 64
@@ -230,43 +229,39 @@
     e1[:F, :S] = pick(pay[:F], one_hot_rows(skel[:, :1], pos * S, S), NT)
     e1[F:32, :S] = product(pay[F:], rgbt[...], NT)
     e1[:32, S:] = jnp.zeros((32, INFO), f32)
-    e1[32:48] = ckeep[...]
-    e1[48:64] = c1r[:16]
-    e1[64:96] = c2r[...]
+    for b, ref in enumerate((ckeep, c8, c6, c14)):
+        e1[32 + 16 * b : 48 + 16 * b] = ref[...]
 
 
 CLUSTER_MASKS = (0, 8, 6, 14)
 
 
-def cluster_up(e1, r1, r2, r3, e2, rcbt, skel):
+def cluster_up(e1, r1, e2, rcbt, skel):
     d = lax.axis_index("leaf")
     gk = (d >> 2) & 3
-    for m, ref in enumerate((e1, r1, r2, r3)):
+    for m, ref, at in ((0, e1, 32), (2, e1, 96), (1, r1, 32), (3, r1, 96)):
         for b, mask in enumerate(CLUSTER_MASKS):
             row = pl.multiple_of(((d & 15) ^ mask ^ m) * 16, 16)
-            rcbt[pl.ds(row, 16), :] = ref[32 + 16 * b : 48 + 16 * b, :S]
-            skel[pl.ds(row, 16), :] = ref[32 + 16 * b : 48 + 16 * b, S:]
-    group = e1[:32, :S] + r1[:32, :S] + (r2[:32, :S] + r3[:32, :S])
+            rows = slice(at + 16 * b, at + 16 * b + 16)
+            rcbt[pl.ds(row, 16), :] = ref[rows, :S]
+            skel[pl.ds(row, 16), :] = ref[rows, S:]
+    group = e1[:32, :S] + r1[:32, :S]
     e2[:, :S] = group
     e2[:F, S:] = pick(group[:F], one_hot_rows(skel[:, :1], gk * S, S), NT)
     e2[F:, S:] = product(group[F:], rcbt[...], NT)
 
 
-def cluster_sum(e2, r1, r2, r3, cpay):
-    cpay[...] = e2[:, S:] + r1[:, S:] + (r2[:, S:] + r3[:, S:])
-
-
 def interact(left, other_points, other_weights):
     values = jnp.exp2(dot(left, exponent_rows(other_points, False), NN))
     return product(other_weights, values, NT)
 
 
-def early_field(e2, g1, g2, g3, cpay, c1, c2, side, top):
+def early_field(e2, h, cpay, c1, c2, side, top):
     left = jnp.transpose(exponent_rows(e2[:F, :S], True))
     side[...] = interact(
         left,
-        jnp.concatenate([g1[:F, :S], g2[:F, :S], g3[:F, :S]], 1),
-        jnp.concatenate([g1[F:, :S], g2[F:, :S], g3[F:, :S]], 1),
+        jnp.concatenate([e2[:F, S : 2 * S], h[:F, : 2 * S]], 1),
+        jnp.concatenate([e2[F:, S : 2 * S], h[F:, : 2 * S]], 1),
     )
     left = jnp.transpose(exponent_rows(cpay[:F], True))
     top[...] = interact(
@@ -286,34 +281,34 @@
         )
 
 
-def make_work(info, work, place):
+def work_items(info):
     d = lax.axis_index("leaf")
-    pos = d & 3
-    even8 = 1 - ((d >> 3) & 1)
-    even4 = 1 - ((d >> 2) & 1)
-    place[0] = 1 + even8
-    place[1] = 3 + even4
-    place[2] = 0
-    place[3] = 4 - even4
-    place[4] = 2 - even8
-
+    row = lax.broadcasted_iota(jnp.int32, info.shape, 0)
+    lane = lax.broadcasted_iota(jnp.int32, info.shape, 1)
+    owner = info >> 2
+    step = owner - d
+    even8 = (d & 8) == 0
+    even4 = (d & 4) == 0
+    shard = jnp.where((step == 8) == even8, 1, 2)
+    shard = jnp.where(jnp.abs(step) == 4, jnp.where((step == 4) == even4, 3, 4), shard)
+    shard = jnp.where(step == 0, 0, shard)
+    item = ((shard * 4 + (info & 3)) << 4) | row
+    mine = ((owner & 3) == (d & 3)) & (lane < info[:, NBR : NBR + 1])
+    return jnp.where(lane == NBR, info, jnp.where(mine, item, -1))
+
+
+def make_work(items, work, first_leaf, filled):
     def list_leaf(leaf, filled):
-        live = info[leaf, NBR]
-
         def list_slots(step, filled):
-            for u in range(4):
-                slot = step * 4 + u
-                source = info[leaf, slot]
-                owner = source >> 2
-                mine = ((owner & 3) == pos) & (slot < live)
-                shard = place[jnp.where(mine, (owner - d + 8) >> 2, 0)]
-                work[filled] = ((shard * 4 + (source & 3)) << 4) | leaf
-                filled += jnp.where(mine, 1, 0)
+            for u in range(8):
+                item = items[leaf, step * 8 + u]
+                work[filled] = item
+                filled += 1 + (item >> 31)
             return filled
 
-        return lax.fori_loop(0, (live + 3) >> 2, list_slots, filled)
-
-    return lax.fori_loop(0, 16, list_leaf, 0)
+        return lax.fori_loop(0, (items[leaf, NBR] + 7) >> 3, list_slots, filled)
+
+    return lax.fori_loop(first_leaf, first_leaf + 8, list_leaf, filled)
 
 
 def run_tiles(first, last, work, left, right, charge, acc):
@@ -342,13 +337,20 @@
     lax.fori_loop(first + whole * UNROLL, last, single, 0)
 
 
-PARTS = (0, 5, 9, 13, 16)
-
-
-def bounds(count, part):
-    first = ((count * PARTS[part]) >> 4) & -UNROLL
-    last = (count * PARTS[part + 1]) >> 4
-    return first, last if part == len(PARTS) - 2 else last & -UNROLL
+PARTS = (0, 3, 6, 9, 13, 16)
+
+
+def bounds(work, part):
+    given = work[WORK - 2]
+    count = work[WORK - 1]
+
+    def edge(i):
+        if i == len(PARTS) - 1:
+            return count
+        at = ((count * PARTS[i]) >> 4) & -UNROLL
+        return jnp.maximum(at, given) if i == len(PARTS) - 2 else at
+
+    return edge(part), edge(part + 1)
 
 
 def source_rows(ref, shard, left, charge):
@@ -363,39 +365,44 @@
         right[4 * q + l] = exponent_rows(ref[:F, at + l * LEAF : at + (l + 1) * LEAF], False)
 
 
-def near_plan(info, w, x1r, left, right, charge, work, place):
-    count = make_work(info, work, place)
+def near_plan(items, w, x2r, x1r, left, right, charge, work):
+    given = make_work(items, work, 0, 0)
+    count = make_work(items, work, 8, given)
+    work[WORK - 2] = given
     work[WORK - 1] = count
     source_rows(w, 0, left, charge)
-    target_rows(w, 0, 0, right)
-    target_rows(x1r, 0, 1, right)
-
-
-def near_start(work, w8, i8, w4, i4, targets, left0, right0, charge0, acc, left, right, charge):
-    del left0, right0, charge0
+    for q, (ref, at) in enumerate(((x1r, 0), (x1r, SPAN), (w, 0), (x2r, 0))):
+        target_rows(ref, at, q, right)
+
+
+def near_start(work, w8, i8, w4, i4, right, left0, charge0, acc, left, charge):
+    del left0, charge0
     for i, ref in enumerate((w8, i8, w4, i4)):
         source_rows(ref, 1 + i, left, charge)
+    acc[...] = jnp.zeros_like(acc)
+    run_tiles(*bounds(work, 0), work, left, right, charge, acc)
+
+
+def near_more(part):
+    def body(work, left, right, charge, before, acc, *give):
+        del before
+        run_tiles(*bounds(work, part), work, left, right, charge, acc)
+        for ref in give:
+            copy_out(acc, 0, ref)
+
+    return body
+
+
+def copy_out(acc, first, ref):
     for q in range(2):
-        target_rows(targets, q * SPAN, 2 + q, right)
-    acc[...] = jnp.zeros_like(acc)
-    run_tiles(*bounds(work[WORK - 1], 0), work, left, right, charge, acc)
-
-
-def near_more(part):
-    def body(work, left, right, charge, before, acc):
-        del before
-        run_tiles(*bounds(work[WORK - 1], part), work, left, right, charge, acc)
-
-    return body
-
-
-def near_last(work, left, right, charge, before, *parts_acc):
-    *parts, acc = parts_acc
-    acc[...] = before[...]
-    run_tiles(*bounds(work[WORK - 1], len(PARTS) - 2), work, left, right, charge, acc)
-    for q, part in enumerate(parts):
         for l in range(LEAVES_DEV):
-            part[:, l * LEAF : (l + 1) * LEAF] = acc[4 * q + l]
+            ref[q, :, l * LEAF : (l + 1) * LEAF] = acc[first + 4 * q + l]
+
+
+def near_last(work, left, right, charge, before, keep, acc):
+    acc[8:] = before[8:]
+    run_tiles(*bounds(work, len(PARTS) - 2), work, left, right, charge, acc)
+    copy_out(acc, 8, keep)
 
 
 WORK = 16 * NBR + 16
@@ -414,7 +421,7 @@
     cluster_basis,
     cluster_skeleton,
 ):
-    w, x1, urgent, gkeep, ckeep, csend, c1 = call(
+    w, x2, gnext, gkeep, ckeep, c8, c6, c14 = call(
         pack_first,
         (
             out(32, PTS),
@@ -423,7 +430,8 @@
             out(16, 4 * S),
             out(16, BLOCK),
             out(16, BLOCK),
-            out(32, BLOCK),
+            out(16, BLOCK),
+            out(16, BLOCK),
         ),
         (
             points,
@@ -447,52 +455,53 @@
             pltpu.SemaphoreType.DMA((9,)),
         ),
     )
-    x1r = partner(x1, 1)
+    x2r = partner(x2, 2)
+    c8r = partner(c8, 8)
+    c6r = partner(c6, 6)
+    c14r = partner(c14, 14)
     w4r = partner(w, 4)
-    c1r = partner(c1, 8)
     w8r = partner(w, 8)
     i8r = staggered(w, 8)
     i4r = staggered(w, 4)
-    urgent = jnp.concatenate([urgent, x1r[:, SPAN + 4 * S :], x1[:, PTS:SPAN], x1r[:, PTS:SPAN]], 1)
-    targets = jnp.concatenate([x1[:, :SPAN], x1r[:, :SPAN]], 1)
-    urgent = partner(urgent, 2)
-    targets = partner(targets, 2)
+    x1r = partner(
+        jnp.concatenate([x2[:, :SPAN], x2r[:, :SPAN], gnext, x2r[:, SPAN + 4 * S :]], 1), 1
+    )
     (pay,) = call(
         device_up,
         (out(32, S),),
         (w, leaf_basis, device_basis, device_skeleton),
-        hbm=(1, 2),
+        hbm=(1, 2, 3),
         scratch=(
             pltpu.VMEM((PTS, S), f32),
             pltpu.VMEM((LEAVES_DEV * S, S), f32),
-            pltpu.SemaphoreType.DMA((LEAVES_DEV + 1,)),
+            pltpu.VMEM((1, S), jnp.int32),
+            pltpu.SemaphoreType.DMA((LEAVES_DEV + 2,)),
         ),
     )
-    c2r = partner(jnp.concatenate([csend, c1r[16:]], 0), 6)
     e1, rgbt, _ = call(
         group_up,
         (out(96, BLOCK), out(S, S), out(S, 128)),
-        (pay, x1, x1r, urgent, gkeep, ckeep, c1r, c2r),
-    )
-    g1, g2, g3 = (partner(e1, m) for m in (1, 2, 3))
-    e2, rcbt, _ = call(cluster_up, (out(32, 2 * S), out(S, S), out(S, 128)), (e1, g1, g2, g3))
-    h1, h2, h3 = (partner(e2, m) for m in (8, 6, 14))
-    (cpay,) = call(cluster_sum, (out(32, S),), (e2, h1, h2, h3))
+        (pay, x2, x2r, x1r, gkeep, ckeep, c8r, c6r, c14r),
+    )
+    g2 = partner(e1, 2)
+    e1 = jnp.concatenate([e1[:32] + g2[:32], e1[32:], g2[32:]], 0)
+    g1 = partner(e1, 1)
+    e2, rcbt, _ = call(cluster_up, (out(32, 2 * S), out(S, S), out(S, 128)), (e1, g1))
+    h8 = partner(e2, 8)
+    e2 = jnp.concatenate([e2[:, :S], h8[:, :S], e2[:, S:] + h8[:, S:]], 1)
+    h6 = partner(e2, 6)
+    cpay = e2[:, 2 * S :] + h6[:, 2 * S :]
     c1 = partner(cpay, 24)
     pair = jnp.concatenate([cpay, c1], 1)
     c2 = partner(pair, 32)
     c3 = partner(jnp.concatenate([pair, c2], 1), 96)
-    side, top = call(early_field, (out(16, S), out(16, S)), (e2, h1, h2, h3, cpay, c1, c2))
+    side, top = call(early_field, (out(16, S), out(16, S)), (e2, h6, cpay, c1, c2))
 
     info = jnp.concatenate(
-        [
-            x1[:4, PTS:SPAN],
-            x1r[:4, PTS:SPAN],
-            urgent[:4, 8 * S : 8 * S + INFO],
-            urgent[:4, 8 * S + INFO :],
-        ],
+        [x1r[:4, PTS:SPAN], x1r[:4, SPAN + PTS : 2 * SPAN], x2[:4, PTS:SPAN], x2r[:4, PTS:SPAN]],
         0,
-    ).astype(jnp.int32)
+    )
+    items = work_items(info.astype(jnp.int32))
     rows = (
         jax.ShapeDtypeStruct((20, LEAF, 128), bf16),
         jax.ShapeDtypeStruct((16, 128, LEAF), bf16),
@@ -501,40 +510,38 @@
     left, right, charge, work = call(
         near_plan,
         (*rows, jax.ShapeDtypeStruct((WORK,), jnp.int32)),
-        (info, w, x1r),
+        (items, w, x2r, x1r),
         smem=(0,),
         smem_outs=(3,),
-        scratch=(pltpu.SMEM((8,), jnp.int32),),
-    )
-    acc, left, right, charge = call(
+    )
+    acc, left, charge = call(
         near_start,
-        (out(16, R, LEAF), *rows),
-        (work, w8r, i8r, w4r, i4r, targets, left, right, charge),
+        (out(16, R, LEAF), rows[0], rows[2]),
+        (work, w8r, i8r, w4r, i4r, right, left, charge),
         smem=(0,),
-        aliases={6: 1, 7: 2, 8: 3},
+        aliases={6: 1, 7: 2},
     )
     for part in range(1, len(PARTS) - 2):
-        (acc,) = call(
+        acc, *give = call(
             near_more(part),
-            (out(16, R, LEAF),),
+            (out(16, R, LEAF),) + (out(2, R, PTS),) * (part == len(PARTS) - 3),
             (work, left, right, charge, acc),
             smem=(0,),
             aliases={4: 0},
         )
-    n0, n1, n2, n3 = call(
+    got = partner(give[0], 1)
+    (keep,) = call(
         near_last,
-        (out(R, PTS),) * 4,
+        (out(2, R, PTS),),
         (work, left, right, charge, acc),
         smem=(0,),
         scratch=(pltpu.VMEM((16, R, LEAF), f32),),
     )
-    n3 = partner(n3, 3)
-    n2 = partner(n2, 2)
-    n1 = partner(n1, 1)
+    near = keep[0] + got[0] + partner(keep[1] + got[1], 2)
     (far,) = call(
         downward, (out(16, PTS),), (cpay, c3, side, top, rcbt, rgbt, device_basis, leaf_basis)
     )
-    return n0 + n1 + (n2 + n3) + far
+    return near + far
 
 
 def solution(mesh):

time: 89.3 us -> 86.4 us (0.968)
  the two profiles are of different devices: /device:TPU:9 before, /device:TPU:0 now
where the time goes in v2:
time: 86.4 us; the launch traced here: 86.2 us
  starting transfers between devices  36 us (42%)
  Pallas kernels  24.7 us (29%)
  waiting for transfers between devices  24.1 us (28%)
  other arithmetic  0.91 us (1%)
    ppermute x16, starting transfers between devices, partner(): lax.ppermute(value, 'leaf', [(source, source ^ mask) for source in range(...  34.7 us
    pallas_call x12, Pallas kernels, call(): pl.pallas_call(body, out_shape=tuple(outs), in_specs=[pl.BlockSpec(memory...  24.7 us
    ppermute x16, waiting for transfers between devices, partner(): lax.ppermute(value, 'leaf', [(source, source ^ mask) for source in range(...  24.1 us
  transfers between devices with their start and end apart: 18, of which 6 were waited for; matrix products, arithmetic and copies ran while one was open for 0% of the time, Pallas kernels for 26%

profile of v2, /device:TPU:0, one launch (start us, length us, event | category | flops | bytes accessed | tf_op | source)
XLA Modules:
  0.0 86.2 jit_solution(16815674734025443260)
XLA Ops:
  0.0 1.3 %shard_map.109 = (f32[32,2048]{1,0:T(8,128)S(1)}, f32[16,4224]{1,0:T(8,128)S(1)}, f32[16,1024]{1,0:T(8,128)S(1)}, f32[16,1024]{1,0:T(8,128)S(1)}, f32[16,384]{1,...) custom-call(f32[16,2048]{1,0:T(8,128)} %points.1, f32[16,2048]{1,0:T(8,128)} %charges.1, ...), custom_call_target="tpu_custom_call" | custom-call | tf_op jit(solution)/shard_map/pallas_call | solution.py:53
  1.3 1.7 %collective-permute-start = (f32[16,4224]{1,0:T(8,128)S(1)}, f32[16,4224]{1,0:T(8,128)S(1)}, u32[]{:S(2)}, u32[]{:S(2)}) collective-permute-start(f32[16,4224]{1,0:T(8,128)S(1)} %get-tuple-element.28.x2), channel_id=1, source_target_pairs={{0,2},{1,3},{2,0},{3,1},{4,6},{5,7},{6,4},{7,5},{8,10},{9,11},{10,... | collective-permute-start | bytes 811016 | tf_op jit(solution)/shard_map/ppermute | solution.py:30
  3.0 6.5 %collective-permute-done.x2r = f32[16,4224]{1,0:T(8,128)S(1)} collective-permute-done((f32[16,4224]{1,0:T(8,128)S(1)}, f32[16,4224]{1,0:T(8,128)S(1)}, u32[]{:S(2)}, u32[]{:S(2)}) %collective-permute-start) | collective-permute-done | bytes 270368 | tf_op jit(solution)/shard_map/ppermute | solution.py:30
  9.6 2.2 %collective-permute-start.8 = (f32[16,384]{1,0:T(8,128)S(1)}, f32[16,384]{1,0:T(8,128)S(1)}, u32[]{:S(2)}, u32[]{:S(2)}) collective-permute-start(f32[16,384]{1,0:T(8,128)S(1)} %get-tuple-element.42), channel_id=1, source_target_pairs={{0,8},{1,9},{2,10},{3,11},{4,12},{5,13},{6,14},{7,15},{8,0},{9,1},... | collective-permute-start | bytes 73736 | tf_op jit(solution)/shard_map/ppermute | solution.py:30
  11.8 2.8 %collective-permute-start.9 = (f32[16,384]{1,0:T(8,128)S(1)}, f32[16,384]{1,0:T(8,128)S(1)}, u32[]{:S(2)}, u32[]{:S(2)}) collective-permute-start(f32[16,384]{1,0:T(8,128)S(1)} %get-tuple-element.43), channel_id=1, source_target_pairs={{0,6},{1,7},{2,4},{3,5},{4,2},{5,3},{6,0},{7,1},{8,14},{9,15},{10,... | collective-permute-start | bytes 73736 | tf_op jit(solution)/shard_map/ppermute | solution.py:30
  14.6 2.5 %shard_map.116.pay = f32[32,256]{1,0:T(8,128)S(1)} custom-call(f32[32,2048]{1,0:T(8,128)S(1)} %get-tuple-element.30.w, f32[2048,256]{1,0:T(8,128)} %leaf.1, f32[1024,256]{1,0:T(8,128)} %device.1, s32[1,256]{1,0:T(1,128)} %skeleton_hbm.1), custom_call_target="tpu_custom_call" | custom-call | tf_op jit(solution)/shard_map/pallas_call | solution.py:53
  17.1 3.4 %collective-permute-done.10.c14 = f32[16,384]{1,0:T(8,128)S(1)} collective-permute-done((f32[16,384]{1,0:T(8,128)S(1)}, f32[16,384]{1,0:T(8,128)S(1)}, u32[]{:S(2)}, u32[]{:S(2)}) %collective-permute-start.10) | collective-permute-done | bytes 24608 | tf_op jit(solution)/shard_map/ppermute | solution.py:30
  20.5 0.8 shard_map.117
  22.0 4.4 %collective-permute-start.4 = (f32[32,2048]{1,0:T(8,128)S(1)}, f32[32,2048]{1,0:T(8,128)S(1)}, u32[]{:S(2)}, u32[]{:S(2)}) collective-permute-start(f32[32,2048]{1,0:T(8,128)S(1)} %get-tuple-element.30.w), channel_id=1, source_target_pairs={{0,4},{1,5},{2,6},{3,7},{4,0},{5,1},{6,2},{7,3},{8,12},{9,13},{10,... | collective-permute-start | bytes 786440 | tf_op jit(solution)/shard_map/ppermute | solution.py:30
  27.0 5.1 %collective-permute-start.2 = (f32[32,2048]{1,0:T(8,128)S(1)}, f32[32,2048]{1,0:T(8,128)S(1)}, u32[]{:S(2)}, u32[]{:S(2)}) collective-permute-start(f32[32,2048]{1,0:T(8,128)S(1)} %get-tuple-element.30.w), channel_id=1, source_target_pairs={{0,8},{1,9},{2,10},{3,11},{4,12},{5,13},{6,14},{7,15},{8,0},{9,1},... | collective-permute-start | bytes 786440 | tf_op jit(solution)/shard_map/ppermute | solution.py:30
  32.4 1.4 %collective-permute-done.12.r1 = f32[160,384]{1,0:T(8,128)S(1)} collective-permute-done((f32[160,384]{1,0:T(8,128)S(1)}, f32[160,384]{1,0:T(8,128)S(1)}, u32[]{:S(2)}, u32[]{:S(2)}) %collective-permute-start.12) | collective-permute-done | bytes 245792 | tf_op jit(solution)/shard_map/ppermute | solution.py:30
  34.7 4.2 %collective-permute-done.13 = f32[32,512]{1,0:T(8,128)S(1)} collective-permute-done((f32[32,512]{1,0:T(8,128)S(1)}, f32[32,512]{1,0:T(8,128)S(1)}, u32[]{:S(2)}, u32[]{:S(2)}) %collective-permute-start.13) | collective-permute-done | bytes 65568 | tf_op jit(solution)/shard_map/ppermute | solution.py:30
  38.9 2.5 %collective-permute-start.14 = (f32[32,768]{1,0:T(8,128)S(1)}, f32[32,768]{1,0:T(8,128)S(1)}, u32[]{:S(2)}, u32[]{:S(2)}) collective-permute-start(f32[32,768]{1,0:T(8,128)S(1)} %pad_maximum_fusion.3.e2), channel_id=1, source_target_pairs={{0,6},{1,7},{2,4},{3,5},{4,2},{5,3},{6,0},{7,1},{8,14},{9,15},{10,... | collective-permute-start | bytes 294920 | tf_op jit(solution)/shard_map/ppermute | solution.py:30
  41.6 3.2 %collective-permute-done.14.h = f32[32,768]{1,0:T(8,128)S(1)} collective-permute-done((f32[32,768]{1,0:T(8,128)S(1)}, f32[32,768]{1,0:T(8,128)S(1)}, u32[]{:S(2)}, u32[]{:S(2)}) %collective-permute-start.14) | collective-permute-done | bytes 98336 | tf_op jit(solution)/shard_map/ppermute | solution.py:30
  44.8 4.3 %collective-permute-start.15 = (f32[32,256]{1,0:T(8,128)S(1)}, f32[32,256]{1,0:T(8,128)S(1)}, u32[]{:S(2)}, u32[]{:S(2)}) collective-permute-start(f32[32,256]{1,0:T(8,128)S(1)} %slice_add_fusion.3.cpay), channel_id=1, source_target_pairs={{0,24},{1,25},{2,26},{3,27},{4,28},{5,29},{6,30},{7,31},{8,16},{9,... | collective-permute-start | bytes 98312 | tf_op jit(solution)/shard_map/ppermute | solution.py:30
  49.2 2.4 %shard_map.110 = (bf16[20,512,128]{2,1,0:T(8,128)(2,1)S(1)}, bf16[16,128,512]{2,1,0:T(8,128)(2,1)S(1)}, bf16[20,16,512]{2,1,0:T(8,128)(2,1)S(1)}, s32[528]{0:T(1024)S(1)}) custom-call(s32[16,128]{1,0:T(8,128)S(1)} %select_select_fusion.items, f32[32,2048]{1,0:T(8,128)S(1)} %get-tuple-element.30.w, f32[16,4224]{1,0:T(8,128)S(1)} %collective-permute-done.x2r, ...), custom_call_target="tpu_custom_call" | custom-call | tf_op jit(solution)/shard_map/pallas_call | solution.py:53
  51.7 3.1 %shard_map.111 = (f32[16,16,512]{2,1,0:T(8,128)S(1)}, bf16[20,512,128]{2,1,0:T(8,128)(2,1)S(1)}, bf16[20,16,512]{2,1,0:T(8,128)(2,1)S(1)}) custom-call(s32[528]{0:T(1024)S(1)} %get-tuple-element.31.work, f32[32,2048]{1,0:T(8,128)S(1)} %collective-permute-done.2.w8, ...), custom_call_target="tpu_custom_call", output_to_operand_aliasing={{1}: (6, {}), {2}: (7, {})} | custom-call | tf_op jit(solution)/shard_map/pallas_call | solution.py:53
  54.7 2.5 %shard_map.112.before = f32[16,16,512]{2,1,0:T(8,128)S(1)} custom-call(s32[528]{0:T(1024)S(1)} %get-tuple-element.31.work, bf16[20,512,128]{2,1,0:T(8,128)(2,1)S(1)} %get-tuple-element.35.left, bf16[16,128,512]{2,1,0:T(8,128)(2,1)S(1)} %get-tuple-element.32.right, bf16[20,16,512]{2,1,0:T(8,128)(2,1)S(1)} %get-tuple-element.36.charge, ...), custom_call_target="tpu_custom_call", output_to_operand_aliasing={{}: (4, {})} | custom-call | tf_op jit(solution)/shard_map/pallas_call | solution.py:53
  57.2 2.5 %shard_map.113.before = f32[16,16,512]{2,1,0:T(8,128)S(1)} custom-call(s32[528]{0:T(1024)S(1)} %get-tuple-element.31.work, bf16[20,512,128]{2,1,0:T(8,128)(2,1)S(1)} %get-tuple-element.35.left, bf16[16,128,512]{2,1,0:T(8,128)(2,1)S(1)} %get-tuple-element.32.right, bf16[20,16,512]{2,1,0:T(8,128)(2,1)S(1)} %get-tuple-element.36.charge, ...), custom_call_target="tpu_custom_call", output_to_operand_aliasing={{}: (4, {})} | custom-call | tf_op jit(solution)/shard_map/pallas_call | solution.py:53
  59.6 2.5 %shard_map.114 = (f32[16,16,512]{2,1,0:T(8,128)S(1)}, f32[2,16,2048]{2,1,0:T(8,128)S(1)}) custom-call(s32[528]{0:T(1024)S(1)} %get-tuple-element.31.work, bf16[20,512,128]{2,1,0:T(8,128)(2,1)S(1)} %get-tuple-element.35.left, bf16[16,128,512]{2,1,0:T(8,128)(2,1)S(1)} %get-tuple-element.32.right, ...), custom_call_target="tpu_custom_call", output_to_operand_aliasing={{0}: (4, {})} | custom-call | tf_op jit(solution)/shard_map/pallas_call | solution.py:53
  62.3 11.1 %collective-permute-start.16 = (f32[32,512]{1,0:T(8,128)S(1)}, f32[32,512]{1,0:T(8,128)S(1)}, u32[]{:S(2)}, u32[]{:S(2)}) collective-permute-start(f32[32,512]{1,0:T(8,128)S(1)} %pad_maximum_fusion.4), channel_id=1, source_target_pairs={{0,32},{1,33},{2,34},{3,35},{4,36},{5,37},{6,38},{7,39},{8,40},{9,... | collective-permute-start | bytes 196616 | tf_op jit(solution)/shard_map/ppermute | solution.py:30
  73.4 3.5 %shard_map.115 = f32[2,16,2048]{2,1,0:T(8,128)S(1)} custom-call(s32[528]{0:T(1024)S(1)} %get-tuple-element.31.work, bf16[20,512,128]{2,1,0:T(8,128)(2,1)S(1)} %get-tuple-element.35.left, bf16[16,128,512]{2,1,0:T(8,128)(2,1)S(1)} %get-tuple-element.32.right, bf16[20,16,512]{2,1,0:T(8,128)(2,1)S(1)} %get-tuple-element.36.charge, ...), custom_call_target="tpu_custom_call" | custom-call | tf_op jit(solution)/shard_map/pallas_call | solution.py:53
  77.9 5.3 %collective-permute-done.17.c3 = f32[32,1024]{1,0:T(8,128)S(1)} collective-permute-done((f32[32,1024]{1,0:T(8,128)S(1)}, f32[32,1024]{1,0:T(8,128)S(1)}, u32[]{:S(2)}, u32[]{:S(2)}) %collective-permute-start.17) | collective-permute-done | bytes 131104 | tf_op jit(solution)/shard_map/ppermute | solution.py:30
  83.2 2.3 %shard_map.120 = f32[16,2048]{1,0:T(8,128)S(1)} custom-call(f32[32,256]{1,0:T(8,128)S(1)} %slice_add_fusion.3.cpay, f32[32,1024]{1,0:T(8,128)S(1)} %collective-permute-done.17.c3, f32[16,256]{1,0:T(8,128)S(1)} %get-tuple-element.47.side, f32[16,256]{1,0:T(8,128)S(1)} %get-tuple-element.48.top, f32[256,256]{1,0:T(8,128)S(1)} %get-tuple-element.49.rcbt, ...), custom_call_target="tpu_custom_call" | custom-call | tf_op jit(solution)/shard_map/pallas_call | solution.py:53
  (50 shorter events, 4.5 us)
Async XLA Ops:
  1.3 8.2 %collective-permute-start = (f32[16,4224]{1,0:T(8,128)S(1)}, f32[16,4224]{1,0:T(8,128)S(1)}, u32[]{:S(2)}, u32[]{:S(2)}) collective-permute-start(f32[16,4224]{1,0:T(8,128)S(1)} %get-tuple-element.28.x2), channel_id=1, source_target_pairs={{0,2},{1,3},{2,0},{3,1},{4,6},{5,7},{6,4},{7,5},{8,10},{9,11},{10,... | collective-permute-start | bytes 811016 | tf_op jit(solution)/shard_map/ppermute | solution.py:30
  9.5 11.0 %collective-permute-start.1 = (f32[16,6400]{1,0:T(8,128)S(1)}, f32[16,6400]{1,0:T(8,128)S(1)}, u32[]{:S(2)}, u32[]{:S(2)}) collective-permute-start(f32[16,6400]{1,0:T(8,128)S(1)} %pad_maximum_fusion), channel_id=1, source_target_pairs={{0,1},{1,0},{2,3},{3,2},{4,5},{5,4},{6,7},{7,6},{8,9},{9,8},{10,11... | collective-permute-start | bytes 1228808 | tf_op jit(solution)/shard_map/ppermute | solution.py:30
  9.6 7.5 %collective-permute-start.8 = (f32[16,384]{1,0:T(8,128)S(1)}, f32[16,384]{1,0:T(8,128)S(1)}, u32[]{:S(2)}, u32[]{:S(2)}) collective-permute-start(f32[16,384]{1,0:T(8,128)S(1)} %get-tuple-element.42), channel_id=1, source_target_pairs={{0,8},{1,9},{2,10},{3,11},{4,12},{5,13},{6,14},{7,15},{8,0},{9,1},... | collective-permute-start | bytes 73736 | tf_op jit(solution)/shard_map/ppermute | solution.py:30
  11.8 5.3 %collective-permute-start.9 = (f32[16,384]{1,0:T(8,128)S(1)}, f32[16,384]{1,0:T(8,128)S(1)}, u32[]{:S(2)}, u32[]{:S(2)}) collective-permute-start(f32[16,384]{1,0:T(8,128)S(1)} %get-tuple-element.43), channel_id=1, source_target_pairs={{0,6},{1,7},{2,4},{3,5},{4,2},{5,3},{6,0},{7,1},{8,14},{9,15},{10,... | collective-permute-start | bytes 73736 | tf_op jit(solution)/shard_map/ppermute | solution.py:30
  14.6 5.9 %collective-permute-start.10 = (f32[16,384]{1,0:T(8,128)S(1)}, f32[16,384]{1,0:T(8,128)S(1)}, u32[]{:S(2)}, u32[]{:S(2)}) collective-permute-start(f32[16,384]{1,0:T(8,128)S(1)} %get-tuple-element.44), channel_id=1, source_target_pairs={{0,14},{1,15},{2,12},{3,13},{4,10},{5,11},{6,8},{7,9},{8,6},{9,7},... | collective-permute-start | bytes 73736 | tf_op jit(solution)/shard_map/ppermute | solution.py:30
  21.3 10.9 %collective-permute-start.11 = (f32[96,384]{1,0:T(8,128)S(1)}, f32[96,384]{1,0:T(8,128)S(1)}, u32[]{:S(2)}, u32[]{:S(2)}) collective-permute-start(f32[96,384]{1,0:T(8,128)S(1)} %get-tuple-element.45), channel_id=1, source_target_pairs={{0,2},{1,3},{2,0},{3,1},{4,6},{5,7},{6,4},{7,5},{8,10},{9,11},{10,... | collective-permute-start | bytes 442376 | tf_op jit(solution)/shard_map/ppermute | solution.py:30
  21.3 30.3 %collective-permute-start.5 = (f32[32,2048]{1,0:T(8,128)S(1)}, f32[32,2048]{1,0:T(8,128)S(1)}, u32[]{:S(2)}, u32[]{:S(2)}) collective-permute-start(f32[32,2048]{1,0:T(8,128)S(1)} %get-tuple-element.30.w), channel_id=1, source_target_pairs={{0,0},{1,1},{2,2},{3,3},{4,8},{5,9},{6,10},{7,11},{8,4},{9,5},{10,... | collective-permute-start | bytes 786440 | tf_op jit(solution)/shard_map/ppermute | solution.py:41
  22.0 29.6 %collective-permute-start.4 = (f32[32,2048]{1,0:T(8,128)S(1)}, f32[32,2048]{1,0:T(8,128)S(1)}, u32[]{:S(2)}, u32[]{:S(2)}) collective-permute-start(f32[32,2048]{1,0:T(8,128)S(1)} %get-tuple-element.30.w), channel_id=1, source_target_pairs={{0,4},{1,5},{2,6},{3,7},{4,0},{5,1},{6,2},{7,3},{8,12},{9,13},{10,... | collective-permute-start | bytes 786440 | tf_op jit(solution)/shard_map/ppermute | solution.py:30
  26.4 25.3 %collective-permute-start.3 = (f32[32,2048]{1,0:T(8,128)S(1)}, f32[32,2048]{1,0:T(8,128)S(1)}, u32[]{:S(2)}, u32[]{:S(2)}) collective-permute-start(f32[32,2048]{1,0:T(8,128)S(1)} %get-tuple-element.30.w), channel_id=1, source_target_pairs={{0,0},{1,1},{2,2},{3,3},{4,4},{5,5},{6,6},{7,7},{8,16},{9,17},{10,... | collective-permute-start | bytes 786440 | tf_op jit(solution)/shard_map/ppermute | solution.py:41
  27.0 24.6 %collective-permute-start.2 = (f32[32,2048]{1,0:T(8,128)S(1)}, f32[32,2048]{1,0:T(8,128)S(1)}, u32[]{:S(2)}, u32[]{:S(2)}) collective-permute-start(f32[32,2048]{1,0:T(8,128)S(1)} %get-tuple-element.30.w), channel_id=1, source_target_pairs={{0,8},{1,9},{2,10},{3,11},{4,12},{5,13},{6,14},{7,15},{8,0},{9,1},... | collective-permute-start | bytes 786440 | tf_op jit(solution)/shard_map/ppermute | solution.py:30
  32.3 1.6 %collective-permute-start.12 = (f32[160,384]{1,0:T(8,128)S(1)}, f32[160,384]{1,0:T(8,128)S(1)}, u32[]{:S(2)}, u32[]{:S(2)}) collective-permute-start(f32[160,384]{1,0:T(8,128)S(1)} %pad_maximum_fusion.1.e1), channel_id=1, source_target_pairs={{0,1},{1,0},{2,3},{3,2},{4,5},{5,4},{6,7},{7,6},{8,9},{9,8},{10,11... | collective-permute-start | bytes 737288 | tf_op jit(solution)/shard_map/ppermute | solution.py:30
  34.6 4.3 %collective-permute-start.13 = (f32[32,512]{1,0:T(8,128)S(1)}, f32[32,512]{1,0:T(8,128)S(1)}, u32[]{:S(2)}, u32[]{:S(2)}) collective-permute-start(f32[32,512]{1,0:T(8,128)S(1)} %get-tuple-element.46), channel_id=1, source_target_pairs={{0,8},{1,9},{2,10},{3,11},{4,12},{5,13},{6,14},{7,15},{8,0},{9,1},... | collective-permute-start | bytes 196616 | tf_op jit(solution)/shard_map/ppermute | solution.py:30
  38.9 5.9 %collective-permute-start.14 = (f32[32,768]{1,0:T(8,128)S(1)}, f32[32,768]{1,0:T(8,128)S(1)}, u32[]{:S(2)}, u32[]{:S(2)}) collective-permute-start(f32[32,768]{1,0:T(8,128)S(1)} %pad_maximum_fusion.3.e2), channel_id=1, source_target_pairs={{0,6},{1,7},{2,4},{3,5},{4,2},{5,3},{6,0},{7,1},{8,14},{9,15},{10,... | collective-permute-start | bytes 294920 | tf_op jit(solution)/shard_map/ppermute | solution.py:30
  44.8 17.4 %collective-permute-start.15 = (f32[32,256]{1,0:T(8,128)S(1)}, f32[32,256]{1,0:T(8,128)S(1)}, u32[]{:S(2)}, u32[]{:S(2)}) collective-permute-start(f32[32,256]{1,0:T(8,128)S(1)} %slice_add_fusion.3.cpay), channel_id=1, source_target_pairs={{0,24},{1,25},{2,26},{3,27},{4,28},{5,29},{6,30},{7,31},{8,16},{9,... | collective-permute-start | bytes 98312 | tf_op jit(solution)/shard_map/ppermute | solution.py:30
  62.1 14.9 %collective-permute-start.6 = (f32[2,16,2048]{2,1,0:T(8,128)S(1)}, f32[2,16,2048]{2,1,0:T(8,128)S(1)}, u32[]{:S(2)}, u32[]{:S(2)}) collective-permute-start(f32[2,16,2048]{2,1,0:T(8,128)S(1)} %get-tuple-element.39), channel_id=1, source_target_pairs={{0,1},{1,0},{2,3},{3,2},{4,5},{5,4},{6,7},{7,6},{8,9},{9,8},{10,11... | collective-permute-start | bytes 786440 | tf_op jit(solution)/shard_map/ppermute | solution.py:30
  62.3 14.7 %collective-permute-start.16 = (f32[32,512]{1,0:T(8,128)S(1)}, f32[32,512]{1,0:T(8,128)S(1)}, u32[]{:S(2)}, u32[]{:S(2)}) collective-permute-start(f32[32,512]{1,0:T(8,128)S(1)} %pad_maximum_fusion.4), channel_id=1, source_target_pairs={{0,32},{1,33},{2,34},{3,35},{4,36},{5,37},{6,38},{7,39},{8,40},{9,... | collective-permute-start | bytes 196616 | tf_op jit(solution)/shard_map/ppermute | solution.py:30
  73.4 9.8 %copy-start = (f32[2048,256]{1,0:T(8,128)S(1)}, f32[2048,256]{1,0:T(8,128)}, u32[]{:S(2)}) copy-start(f32[2048,256]{1,0:T(8,128)} %leaf.1) | copy-start | bytes 6291460
  73.4 9.8 %copy-start.1 = (f32[1024,256]{1,0:T(8,128)S(1)}, f32[1024,256]{1,0:T(8,128)}, u32[]{:S(2)}) copy-start(f32[1024,256]{1,0:T(8,128)} %device.1) | copy-start | bytes 3145732
  76.9 6.3 %collective-permute-start.17 = (f32[32,1024]{1,0:T(8,128)S(1)}, f32[32,1024]{1,0:T(8,128)S(1)}, u32[]{:S(2)}, u32[]{:S(2)}) collective-permute-start(f32[32,1024]{1,0:T(8,128)S(1)} %pad_maximum_fusion.2), channel_id=1, source_target_pairs={{0,96},{1,97},{2,98},{3,99},{4,100},{5,101},{6,102},{7,103},{8,104... | collective-permute-start | bytes 393224 | tf_op jit(solution)/shard_map/ppermute | solution.py:30
  77.1 8.4 %collective-permute-start.7 = (f32[16,2048]{1,0:T(8,128)S(1)}, f32[16,2048]{1,0:T(8,128)S(1)}, u32[]{:S(2)}, u32[]{:S(2)}) collective-permute-start(f32[16,2048]{1,0:T(8,128)S(1)} %fusion), channel_id=1, source_target_pairs={{0,2},{1,3},{2,0},{3,1},{4,6},{5,7},{6,4},{7,5},{8,10},{9,11},{10,... | collective-permute-start | bytes 393224 | tf_op jit(solution)/shard_map/ppermute | solution.py:30

commit v3 on v2

--- a/solution.py
+++ b/solution.py
@@ -269,16 +269,16 @@
     )
 
 
-def downward(cpay, c3, side, top, rcbt, rgbt, device, leaf, far):
+def downward(cpay, c3, side, top, rcbt, rgbt, device, leaf, keep, got, rest, far):
     left = jnp.transpose(exponent_rows(cpay[:F], True))
     total = top[...] + interact(left, c3[:F], c3[F:])
     down_group = side[...] + product(total, rcbt[...], NN)
     down_device = product(down_group, rgbt[...], NN)
     down_leaves = product(down_device, device[...], NT)
     for l in range(LEAVES_DEV):
-        far[:, l * LEAF : (l + 1) * LEAF] = product(
-            down_leaves[:, l * S : (l + 1) * S], leaf[l * LEAF : (l + 1) * LEAF], NT
-        )
+        cols = slice(l * LEAF, (l + 1) * LEAF)
+        near = keep[0, :, cols] + got[0, :, cols] + rest[:, cols]
+        far[:, cols] = near + product(down_leaves[:, l * S : (l + 1) * S], leaf[cols], NT)
 
 
 def work_items(info):
@@ -537,11 +537,13 @@
         smem=(0,),
         scratch=(pltpu.VMEM((16, R, LEAF), f32),),
     )
-    near = keep[0] + got[0] + partner(keep[1] + got[1], 2)
-    (far,) = call(
-        downward, (out(16, PTS),), (cpay, c3, side, top, rcbt, rgbt, device_basis, leaf_basis)
-    )
-    return near + far
+    rest = partner(keep[1] + got[1], 2)
+    (total,) = call(
+        downward,
+        (out(16, PTS),),
+        (cpay, c3, side, top, rcbt, rgbt, device_basis, leaf_basis, keep, got, rest),
+    )
+    return total
 
 
 def solution(mesh):

time: 86.4 us -> 84.7 us (0.980)
  starting transfers between devices: 36 us -> 34.8 us
    ppermute x16, starting transfers between devices: 34.7 us -> 33.4 us  [partner(): lax.ppermute(value, 'leaf', [(source, source ^ mask) for source in range(...]
  transfers between devices with their start and end apart: 18 -> 18, of which waited for: 6 -> 7; matrix products, arithmetic and copies ran while one was open for 0% -> 0% of each run, Pallas kernels for 26% -> 24%
where the time goes in v3:
time: 84.7 us; the launch traced here: 84.5 us
  starting transfers between devices  34.8 us (41%)
  Pallas kernels  25.3 us (30%)
  waiting for transfers between devices  23.8 us (28%)
    ppermute x16, starting transfers between devices, partner(): lax.ppermute(value, 'leaf', [(source, source ^ mask) for source in range(...  33.4 us
    pallas_call x12, Pallas kernels, call(): pl.pallas_call(body, out_shape=tuple(outs), in_specs=[pl.BlockSpec(memory...  25.3 us
    ppermute x16, waiting for transfers between devices, partner(): lax.ppermute(value, 'leaf', [(source, source ^ mask) for source in range(...  23.8 us
  transfers between devices with their start and end apart: 18, of which 7 were waited for; matrix products, arithmetic and copies ran while one was open for 0% of the time, Pallas kernels for 24%

profile of v3, /device:TPU:0, one launch (start us, length us, event | category | flops | bytes accessed | tf_op | source)
XLA Modules:
  0.0 84.5 jit_solution(12755442685532321526)
XLA Ops:
  0.0 1.3 %shard_map.109 = (f32[32,2048]{1,0:T(8,128)S(1)}, f32[16,4224]{1,0:T(8,128)S(1)}, f32[16,1024]{1,0:T(8,128)S(1)}, f32[16,1024]{1,0:T(8,128)S(1)}, f32[16,384]{1,...) custom-call(f32[16,2048]{1,0:T(8,128)} %points.1, f32[16,2048]{1,0:T(8,128)} %charges.1, ...), custom_call_target="tpu_custom_call" | custom-call | tf_op jit(solution)/shard_map/pallas_call | solution.py:53
  1.3 1.7 %collective-permute-start = (f32[16,4224]{1,0:T(8,128)S(1)}, f32[16,4224]{1,0:T(8,128)S(1)}, u32[]{:S(2)}, u32[]{:S(2)}) collective-permute-start(f32[16,4224]{1,0:T(8,128)S(1)} %get-tuple-element.29.x2), channel_id=1, source_target_pairs={{0,2},{1,3},{2,0},{3,1},{4,6},{5,7},{6,4},{7,5},{8,10},{9,11},{10,... | collective-permute-start | bytes 811016 | tf_op jit(solution)/shard_map/ppermute | solution.py:30
  3.0 6.5 %collective-permute-done.x2r = f32[16,4224]{1,0:T(8,128)S(1)} collective-permute-done((f32[16,4224]{1,0:T(8,128)S(1)}, f32[16,4224]{1,0:T(8,128)S(1)}, u32[]{:S(2)}, u32[]{:S(2)}) %collective-permute-start) | collective-permute-done | bytes 270368 | tf_op jit(solution)/shard_map/ppermute | solution.py:30
  9.6 2.2 %collective-permute-start.2 = (f32[16,384]{1,0:T(8,128)S(1)}, f32[16,384]{1,0:T(8,128)S(1)}, u32[]{:S(2)}, u32[]{:S(2)}) collective-permute-start(f32[16,384]{1,0:T(8,128)S(1)} %get-tuple-element.33), channel_id=1, source_target_pairs={{0,8},{1,9},{2,10},{3,11},{4,12},{5,13},{6,14},{7,15},{8,0},{9,1},... | collective-permute-start | bytes 73736 | tf_op jit(solution)/shard_map/ppermute | solution.py:30
  11.8 2.8 %collective-permute-start.3 = (f32[16,384]{1,0:T(8,128)S(1)}, f32[16,384]{1,0:T(8,128)S(1)}, u32[]{:S(2)}, u32[]{:S(2)}) collective-permute-start(f32[16,384]{1,0:T(8,128)S(1)} %get-tuple-element.34), channel_id=1, source_target_pairs={{0,6},{1,7},{2,4},{3,5},{4,2},{5,3},{6,0},{7,1},{8,14},{9,15},{10,... | collective-permute-start | bytes 73736 | tf_op jit(solution)/shard_map/ppermute | solution.py:30
  14.6 2.5 %shard_map.110.pay = f32[32,256]{1,0:T(8,128)S(1)} custom-call(f32[32,2048]{1,0:T(8,128)S(1)} %get-tuple-element.28.w, f32[2048,256]{1,0:T(8,128)} %leaf.1, f32[1024,256]{1,0:T(8,128)} %device.1, s32[1,256]{1,0:T(1,128)} %skeleton_hbm.1), custom_call_target="tpu_custom_call" | custom-call | tf_op jit(solution)/shard_map/pallas_call | solution.py:53
  17.1 3.4 %collective-permute-done.4.c14 = f32[16,384]{1,0:T(8,128)S(1)} collective-permute-done((f32[16,384]{1,0:T(8,128)S(1)}, f32[16,384]{1,0:T(8,128)S(1)}, u32[]{:S(2)}, u32[]{:S(2)}) %collective-permute-start.4) | collective-permute-done | bytes 24608 | tf_op jit(solution)/shard_map/ppermute | solution.py:30
  22.0 4.4 %collective-permute-start.14 = (f32[32,2048]{1,0:T(8,128)S(1)}, f32[32,2048]{1,0:T(8,128)S(1)}, u32[]{:S(2)}, u32[]{:S(2)}) collective-permute-start(f32[32,2048]{1,0:T(8,128)S(1)} %get-tuple-element.28.w), channel_id=1, source_target_pairs={{0,4},{1,5},{2,6},{3,7},{4,0},{5,1},{6,2},{7,3},{8,12},{9,13},{10,... | collective-permute-start | bytes 786440 | tf_op jit(solution)/shard_map/ppermute | solution.py:30
  27.0 5.1 %collective-permute-start.12 = (f32[32,2048]{1,0:T(8,128)S(1)}, f32[32,2048]{1,0:T(8,128)S(1)}, u32[]{:S(2)}, u32[]{:S(2)}) collective-permute-start(f32[32,2048]{1,0:T(8,128)S(1)} %get-tuple-element.28.w), channel_id=1, source_target_pairs={{0,8},{1,9},{2,10},{3,11},{4,12},{5,13},{6,14},{7,15},{8,0},{9,1},... | collective-permute-start | bytes 786440 | tf_op jit(solution)/shard_map/ppermute | solution.py:30
  32.4 1.5 %collective-permute-done.6.r1 = f32[160,384]{1,0:T(8,128)S(1)} collective-permute-done((f32[160,384]{1,0:T(8,128)S(1)}, f32[160,384]{1,0:T(8,128)S(1)}, u32[]{:S(2)}, u32[]{:S(2)}) %collective-permute-start.6) | collective-permute-done | bytes 245792 | tf_op jit(solution)/shard_map/ppermute | solution.py:30
  34.9 4.0 %collective-permute-done.7 = f32[32,512]{1,0:T(8,128)S(1)} collective-permute-done((f32[32,512]{1,0:T(8,128)S(1)}, f32[32,512]{1,0:T(8,128)S(1)}, u32[]{:S(2)}, u32[]{:S(2)}) %collective-permute-start.7) | collective-permute-done | bytes 65568 | tf_op jit(solution)/shard_map/ppermute | solution.py:30
  38.9 2.5 %collective-permute-start.8 = (f32[32,768]{1,0:T(8,128)S(1)}, f32[32,768]{1,0:T(8,128)S(1)}, u32[]{:S(2)}, u32[]{:S(2)}) collective-permute-start(f32[32,768]{1,0:T(8,128)S(1)} %pad_maximum_fusion.3.e2), channel_id=1, source_target_pairs={{0,6},{1,7},{2,4},{3,5},{4,2},{5,3},{6,0},{7,1},{8,14},{9,15},{10,... | collective-permute-start | bytes 294920 | tf_op jit(solution)/shard_map/ppermute | solution.py:30
  41.5 2.4 %shard_map.114 = (bf16[20,512,128]{2,1,0:T(8,128)(2,1)S(1)}, bf16[16,128,512]{2,1,0:T(8,128)(2,1)S(1)}, bf16[20,16,512]{2,1,0:T(8,128)(2,1)S(1)}, s32[528]{0:T(1024)S(1)}) custom-call(s32[16,128]{1,0:T(8,128)S(1)} %select_select_fusion.items, f32[32,2048]{1,0:T(8,128)S(1)} %get-tuple-element.28.w, f32[16,4224]{1,0:T(8,128)S(1)} %collective-permute-done.x2r, ...), custom_call_target="tpu_custom_call" | custom-call | tf_op jit(solution)/shard_map/pallas_call | solution.py:53
  43.9 3.1 %shard_map.115 = (f32[16,16,512]{2,1,0:T(8,128)S(1)}, bf16[20,512,128]{2,1,0:T(8,128)(2,1)S(1)}, bf16[20,16,512]{2,1,0:T(8,128)(2,1)S(1)}) custom-call(s32[528]{0:T(1024)S(1)} %get-tuple-element.42.work, f32[32,2048]{1,0:T(8,128)S(1)} %collective-permute-done.12.w8, ...), custom_call_target="tpu_custom_call", output_to_operand_aliasing={{1}: (6, {}), {2}: (7, {})} | custom-call | tf_op jit(solution)/shard_map/pallas_call | solution.py:53
  47.0 2.5 %shard_map.116.before = f32[16,16,512]{2,1,0:T(8,128)S(1)} custom-call(s32[528]{0:T(1024)S(1)} %get-tuple-element.42.work, bf16[20,512,128]{2,1,0:T(8,128)(2,1)S(1)} %get-tuple-element.46.left, bf16[16,128,512]{2,1,0:T(8,128)(2,1)S(1)} %get-tuple-element.43.right, bf16[20,16,512]{2,1,0:T(8,128)(2,1)S(1)} %get-tuple-element.47.charge, ...), custom_call_target="tpu_custom_call", output_to_operand_aliasing={{}: (4, {})} | custom-call | tf_op jit(solution)/shard_map/pallas_call | solution.py:53
  49.4 2.5 %shard_map.117.before = f32[16,16,512]{2,1,0:T(8,128)S(1)} custom-call(s32[528]{0:T(1024)S(1)} %get-tuple-element.42.work, bf16[20,512,128]{2,1,0:T(8,128)(2,1)S(1)} %get-tuple-element.46.left, bf16[16,128,512]{2,1,0:T(8,128)(2,1)S(1)} %get-tuple-element.43.right, bf16[20,16,512]{2,1,0:T(8,128)(2,1)S(1)} %get-tuple-element.47.charge, ...), custom_call_target="tpu_custom_call", output_to_operand_aliasing={{}: (4, {})} | custom-call | tf_op jit(solution)/shard_map/pallas_call | solution.py:53
  51.9 2.5 %shard_map.118 = (f32[16,16,512]{2,1,0:T(8,128)S(1)}, f32[2,16,2048]{2,1,0:T(8,128)S(1)}) custom-call(s32[528]{0:T(1024)S(1)} %get-tuple-element.42.work, bf16[20,512,128]{2,1,0:T(8,128)(2,1)S(1)} %get-tuple-element.46.left, bf16[16,128,512]{2,1,0:T(8,128)(2,1)S(1)} %get-tuple-element.43.right, ...), custom_call_target="tpu_custom_call", output_to_operand_aliasing={{0}: (4, {})} | custom-call | tf_op jit(solution)/shard_map/pallas_call | solution.py:53
  54.5 3.0 %collective-permute-start.9 = (f32[32,256]{1,0:T(8,128)S(1)}, f32[32,256]{1,0:T(8,128)S(1)}, u32[]{:S(2)}, u32[]{:S(2)}) collective-permute-start(f32[32,256]{1,0:T(8,128)S(1)} %slice_add_fusion.2.cpay), channel_id=1, source_target_pairs={{0,24},{1,25},{2,26},{3,27},{4,28},{5,29},{6,30},{7,31},{8,16},{9,... | collective-permute-start | bytes 98312 | tf_op jit(solution)/shard_map/ppermute | solution.py:30
  57.5 3.4 %shard_map.119.keep = f32[2,16,2048]{2,1,0:T(8,128)S(1)} custom-call(s32[528]{0:T(1024)S(1)} %get-tuple-element.42.work, bf16[20,512,128]{2,1,0:T(8,128)(2,1)S(1)} %get-tuple-element.46.left, bf16[16,128,512]{2,1,0:T(8,128)(2,1)S(1)} %get-tuple-element.43.right, bf16[20,16,512]{2,1,0:T(8,128)(2,1)S(1)} %get-tuple-element.47.charge, ...), custom_call_target="tpu_custom_call" | custom-call | tf_op jit(solution)/shard_map/pallas_call | solution.py:53
  60.9 11.3 %collective-permute-start.10 = (f32[32,512]{1,0:T(8,128)S(1)}, f32[32,512]{1,0:T(8,128)S(1)}, u32[]{:S(2)}, u32[]{:S(2)}) collective-permute-start(f32[32,512]{1,0:T(8,128)S(1)} %pad_maximum_fusion.4), channel_id=1, source_target_pairs={{0,32},{1,33},{2,34},{3,35},{4,36},{5,37},{6,38},{7,39},{8,40},{9,... | collective-permute-start | bytes 196616 | tf_op jit(solution)/shard_map/ppermute | solution.py:30
  72.3 2.6 %collective-permute-done.10.c2 = f32[32,512]{1,0:T(8,128)S(1)} collective-permute-done((f32[32,512]{1,0:T(8,128)S(1)}, f32[32,512]{1,0:T(8,128)S(1)}, u32[]{:S(2)}, u32[]{:S(2)}) %collective-permute-start.10) | collective-permute-done | bytes 65568 | tf_op jit(solution)/shard_map/ppermute | solution.py:30
  75.8 2.1 %collective-permute-done.17.rest = f32[16,2048]{1,0:T(8,128)S(1)} collective-permute-done((f32[16,2048]{1,0:T(8,128)S(1)}, f32[16,2048]{1,0:T(8,128)S(1)}, u32[]{:S(2)}, u32[]{:S(2)}) %collective-permute-start.17) | collective-permute-done | bytes 131104 | tf_op jit(solution)/shard_map/ppermute | solution.py:30
  77.9 3.7 %collective-permute-done.11.c3 = f32[32,1024]{1,0:T(8,128)S(1)} collective-permute-done((f32[32,1024]{1,0:T(8,128)S(1)}, f32[32,1024]{1,0:T(8,128)S(1)}, u32[]{:S(2)}, u32[]{:S(2)}) %collective-permute-start.11) | collective-permute-done | bytes 131104 | tf_op jit(solution)/shard_map/ppermute | solution.py:30
  81.6 3.0 %shard_map.120 = f32[16,2048]{1,0:T(8,128)} custom-call(f32[32,256]{1,0:T(8,128)S(1)} %slice_add_fusion.2.cpay, f32[32,1024]{1,0:T(8,128)S(1)} %collective-permute-done.11.c3, f32[16,256]{1,0:T(8,128)S(1)} %get-tuple-element.38.side, f32[16,256]{1,0:T(8,128)S(1)} %get-tuple-element.39.top, f32[256,256]{1,0:T(8,128)S(1)} %get-tuple-element.40.rcbt, ...), custom_call_target="tpu_custom_call" | custom-call | tf_op jit(solution)/shard_map/pallas_call | solution.py:53
  (49 shorter events, 4.5 us)
Async XLA Ops:
  1.3 8.2 %collective-permute-start = (f32[16,4224]{1,0:T(8,128)S(1)}, f32[16,4224]{1,0:T(8,128)S(1)}, u32[]{:S(2)}, u32[]{:S(2)}) collective-permute-start(f32[16,4224]{1,0:T(8,128)S(1)} %get-tuple-element.29.x2), channel_id=1, source_target_pairs={{0,2},{1,3},{2,0},{3,1},{4,6},{5,7},{6,4},{7,5},{8,10},{9,11},{10,... | collective-permute-start | bytes 811016 | tf_op jit(solution)/shard_map/ppermute | solution.py:30
  9.5 11.0 %collective-permute-start.1 = (f32[16,6400]{1,0:T(8,128)S(1)}, f32[16,6400]{1,0:T(8,128)S(1)}, u32[]{:S(2)}, u32[]{:S(2)}) collective-permute-start(f32[16,6400]{1,0:T(8,128)S(1)} %pad_maximum_fusion), channel_id=1, source_target_pairs={{0,1},{1,0},{2,3},{3,2},{4,5},{5,4},{6,7},{7,6},{8,9},{9,8},{10,11... | collective-permute-start | bytes 1228808 | tf_op jit(solution)/shard_map/ppermute | solution.py:30
  9.6 7.5 %collective-permute-start.2 = (f32[16,384]{1,0:T(8,128)S(1)}, f32[16,384]{1,0:T(8,128)S(1)}, u32[]{:S(2)}, u32[]{:S(2)}) collective-permute-start(f32[16,384]{1,0:T(8,128)S(1)} %get-tuple-element.33), channel_id=1, source_target_pairs={{0,8},{1,9},{2,10},{3,11},{4,12},{5,13},{6,14},{7,15},{8,0},{9,1},... | collective-permute-start | bytes 73736 | tf_op jit(solution)/shard_map/ppermute | solution.py:30
  11.8 5.3 %collective-permute-start.3 = (f32[16,384]{1,0:T(8,128)S(1)}, f32[16,384]{1,0:T(8,128)S(1)}, u32[]{:S(2)}, u32[]{:S(2)}) collective-permute-start(f32[16,384]{1,0:T(8,128)S(1)} %get-tuple-element.34), channel_id=1, source_target_pairs={{0,6},{1,7},{2,4},{3,5},{4,2},{5,3},{6,0},{7,1},{8,14},{9,15},{10,... | collective-permute-start | bytes 73736 | tf_op jit(solution)/shard_map/ppermute | solution.py:30
  14.6 5.9 %collective-permute-start.4 = (f32[16,384]{1,0:T(8,128)S(1)}, f32[16,384]{1,0:T(8,128)S(1)}, u32[]{:S(2)}, u32[]{:S(2)}) collective-permute-start(f32[16,384]{1,0:T(8,128)S(1)} %get-tuple-element.35), channel_id=1, source_target_pairs={{0,14},{1,15},{2,12},{3,13},{4,10},{5,11},{6,8},{7,9},{8,6},{9,7},... | collective-permute-start | bytes 73736 | tf_op jit(solution)/shard_map/ppermute | solution.py:30
  21.3 10.9 %collective-permute-start.5 = (f32[96,384]{1,0:T(8,128)S(1)}, f32[96,384]{1,0:T(8,128)S(1)}, u32[]{:S(2)}, u32[]{:S(2)}) collective-permute-start(f32[96,384]{1,0:T(8,128)S(1)} %get-tuple-element.36), channel_id=1, source_target_pairs={{0,2},{1,3},{2,0},{3,1},{4,6},{5,7},{6,4},{7,5},{8,10},{9,11},{10,... | collective-permute-start | bytes 442376 | tf_op jit(solution)/shard_map/ppermute | solution.py:30
  21.3 22.6 %collective-permute-start.15 = (f32[32,2048]{1,0:T(8,128)S(1)}, f32[32,2048]{1,0:T(8,128)S(1)}, u32[]{:S(2)}, u32[]{:S(2)}) collective-permute-start(f32[32,2048]{1,0:T(8,128)S(1)} %get-tuple-element.28.w), channel_id=1, source_target_pairs={{0,0},{1,1},{2,2},{3,3},{4,8},{5,9},{6,10},{7,11},{8,4},{9,5},{10,... | collective-permute-start | bytes 786440 | tf_op jit(solution)/shard_map/ppermute | solution.py:41
  22.0 21.9 %collective-permute-start.14 = (f32[32,2048]{1,0:T(8,128)S(1)}, f32[32,2048]{1,0:T(8,128)S(1)}, u32[]{:S(2)}, u32[]{:S(2)}) collective-permute-start(f32[32,2048]{1,0:T(8,128)S(1)} %get-tuple-element.28.w), channel_id=1, source_target_pairs={{0,4},{1,5},{2,6},{3,7},{4,0},{5,1},{6,2},{7,3},{8,12},{9,13},{10,... | collective-permute-start | bytes 786440 | tf_op jit(solution)/shard_map/ppermute | solution.py:30
  26.4 17.5 %collective-permute-start.13 = (f32[32,2048]{1,0:T(8,128)S(1)}, f32[32,2048]{1,0:T(8,128)S(1)}, u32[]{:S(2)}, u32[]{:S(2)}) collective-permute-start(f32[32,2048]{1,0:T(8,128)S(1)} %get-tuple-element.28.w), channel_id=1, source_target_pairs={{0,0},{1,1},{2,2},{3,3},{4,4},{5,5},{6,6},{7,7},{8,16},{9,17},{10,... | collective-permute-start | bytes 786440 | tf_op jit(solution)/shard_map/ppermute | solution.py:41
  27.0 16.9 %collective-permute-start.12 = (f32[32,2048]{1,0:T(8,128)S(1)}, f32[32,2048]{1,0:T(8,128)S(1)}, u32[]{:S(2)}, u32[]{:S(2)}) collective-permute-start(f32[32,2048]{1,0:T(8,128)S(1)} %get-tuple-element.28.w), channel_id=1, source_target_pairs={{0,8},{1,9},{2,10},{3,11},{4,12},{5,13},{6,14},{7,15},{8,0},{9,1},... | collective-permute-start | bytes 786440 | tf_op jit(solution)/shard_map/ppermute | solution.py:30
  32.3 1.6 %collective-permute-start.6 = (f32[160,384]{1,0:T(8,128)S(1)}, f32[160,384]{1,0:T(8,128)S(1)}, u32[]{:S(2)}, u32[]{:S(2)}) collective-permute-start(f32[160,384]{1,0:T(8,128)S(1)} %pad_maximum_fusion.1.e1), channel_id=1, source_target_pairs={{0,1},{1,0},{2,3},{3,2},{4,5},{5,4},{6,7},{7,6},{8,9},{9,8},{10,11... | collective-permute-start | bytes 737288 | tf_op jit(solution)/shard_map/ppermute | solution.py:30
  34.6 4.3 %collective-permute-start.7 = (f32[32,512]{1,0:T(8,128)S(1)}, f32[32,512]{1,0:T(8,128)S(1)}, u32[]{:S(2)}, u32[]{:S(2)}) collective-permute-start(f32[32,512]{1,0:T(8,128)S(1)} %get-tuple-element.37), channel_id=1, source_target_pairs={{0,8},{1,9},{2,10},{3,11},{4,12},{5,13},{6,14},{7,15},{8,0},{9,1},... | collective-permute-start | bytes 196616 | tf_op jit(solution)/shard_map/ppermute | solution.py:30
  38.9 15.5 %collective-permute-start.8 = (f32[32,768]{1,0:T(8,128)S(1)}, f32[32,768]{1,0:T(8,128)S(1)}, u32[]{:S(2)}, u32[]{:S(2)}) collective-permute-start(f32[32,768]{1,0:T(8,128)S(1)} %pad_maximum_fusion.3.e2), channel_id=1, source_target_pairs={{0,6},{1,7},{2,4},{3,5},{4,2},{5,3},{6,0},{7,1},{8,14},{9,15},{10,... | collective-permute-start | bytes 294920 | tf_op jit(solution)/shard_map/ppermute | solution.py:30
  54.4 17.8 %collective-permute-start.16 = (f32[2,16,2048]{2,1,0:T(8,128)S(1)}, f32[2,16,2048]{2,1,0:T(8,128)S(1)}, u32[]{:S(2)}, u32[]{:S(2)}) collective-permute-start(f32[2,16,2048]{2,1,0:T(8,128)S(1)} %get-tuple-element.50), channel_id=1, source_target_pairs={{0,1},{1,0},{2,3},{3,2},{4,5},{5,4},{6,7},{7,6},{8,9},{9,8},{10,11... | collective-permute-start | bytes 786440 | tf_op jit(solution)/shard_map/ppermute | solution.py:30
  54.5 6.4 %collective-permute-start.9 = (f32[32,256]{1,0:T(8,128)S(1)}, f32[32,256]{1,0:T(8,128)S(1)}, u32[]{:S(2)}, u32[]{:S(2)}) collective-permute-start(f32[32,256]{1,0:T(8,128)S(1)} %slice_add_fusion.2.cpay), channel_id=1, source_target_pairs={{0,24},{1,25},{2,26},{3,27},{4,28},{5,29},{6,30},{7,31},{8,16},{9,... | collective-permute-start | bytes 98312 | tf_op jit(solution)/shard_map/ppermute | solution.py:30
  57.5 24.1 %copy-start = (f32[2048,256]{1,0:T(8,128)S(1)}, f32[2048,256]{1,0:T(8,128)}, u32[]{:S(2)}) copy-start(f32[2048,256]{1,0:T(8,128)} %leaf.1) | copy-start | bytes 6291460
  57.5 24.1 %copy-start.1 = (f32[1024,256]{1,0:T(8,128)S(1)}, f32[1024,256]{1,0:T(8,128)}, u32[]{:S(2)}) copy-start(f32[1024,256]{1,0:T(8,128)} %device.1) | copy-start | bytes 3145732
  60.9 14.0 %collective-permute-start.10 = (f32[32,512]{1,0:T(8,128)S(1)}, f32[32,512]{1,0:T(8,128)S(1)}, u32[]{:S(2)}, u32[]{:S(2)}) collective-permute-start(f32[32,512]{1,0:T(8,128)S(1)} %pad_maximum_fusion.4), channel_id=1, source_target_pairs={{0,32},{1,33},{2,34},{3,35},{4,36},{5,37},{6,38},{7,39},{8,40},{9,... | collective-permute-start | bytes 196616 | tf_op jit(solution)/shard_map/ppermute | solution.py:30
  72.2 5.7 %collective-permute-start.17 = (f32[16,2048]{1,0:T(8,128)S(1)}, f32[16,2048]{1,0:T(8,128)S(1)}, u32[]{:S(2)}, u32[]{:S(2)}) collective-permute-start(f32[16,2048]{1,0:T(8,128)S(1)} %fusion), channel_id=1, source_target_pairs={{0,2},{1,3},{2,0},{3,1},{4,6},{5,7},{6,4},{7,5},{8,10},{9,11},{10,... | collective-permute-start | bytes 393224 | tf_op jit(solution)/shard_map/ppermute | solution.py:30
  75.0 6.6 %collective-permute-start.11 = (f32[32,1024]{1,0:T(8,128)S(1)}, f32[32,1024]{1,0:T(8,128)S(1)}, u32[]{:S(2)}, u32[]{:S(2)}) collective-permute-start(f32[32,1024]{1,0:T(8,128)S(1)} %pad_maximum_fusion.2), channel_id=1, source_target_pairs={{0,96},{1,97},{2,98},{3,99},{4,100},{5,101},{6,102},{7,103},{8,104... | collective-permute-start | bytes 393224 | tf_op jit(solution)/shard_map/ppermute | solution.py:30
